TPU v7x, 32 devices: a whole 2x2x4 slice. The times are simulated.
32 devices in a mesh: row: 4 (over x, core), col: 8 (over z, y).
Axes of the slice: x: 2, y: 2, z: 4, core: 2. Of those that a mesh axis runs over, the one named last changes fastest.
Arguments:
- object_field: float32 [2, 1024, 2048], P(None, 'row', 'col'), may hold values from -6 to 6
- probe: float32 [2, 128, 128], replicated, may hold values from -6 to 6
- amplitude: bfloat16 [4, 8, 16, 128, 128], P('row', 'col'), may hold values from 0 to 2
- corners: int32 [2, 4, 8, 16], P(None, 'row', 'col'), may hold values from 0 to 255, as said below
- live_count: int32 [4, 8], P('row', 'col'), may hold values from 4 to 16, as said below
Outputs:
- refined_object: float32 [2, 1024, 2048], P(None, 'row', 'col')
- new_probe: float32 [2, 128, 128], replicated
Inputs may be any that keep to these rules, and one draw needn't show every extreme that they name: In the last tile row of the mesh corners[0] is at most 128, and in the last tile column corners[1] is at most 128, so every window lies inside the object. Outside the last tile row, corners[0] of slot 0 is at least 192; outside the last tile column, corners[1] of slot 0 is at least 192. Unused slots carry valid corners. Slots from live_count on are unused. Some tile uses all 16 slots in every draw.
All inputs are finite; a program needn't handle non-finite values.
Results may differ from a plain program's by a relative error of at most 0.0039.
The roundings to bfloat16 on the way count: a program that leaves them out, or rounds other values in their place, can miss the bound.
Values may be sent and summed in bfloat16 or wider, within the bound.
A program may use at most 64 MiB of HBM per device.

v0:
```python
import math

import jax
import jax.numpy as jnp
from jax import lax
from jax.sharding import PartitionSpec as P

BLOCK = 4


def from_behind(value, axis, steps):
    count = lax.axis_size(axis)
    first, last = (max(0, -steps), min(count, count - steps))
    return lax.ppermute(value, axis, [(source, source + steps) for source in range(first, last)])


def dft_tables(window):
    indices = jnp.arange(window, dtype=jnp.int32)
    phase_index = indices[:, None] * indices[None, :] % window
    angles = phase_index.astype(jnp.float32) * (2.0 * math.pi / window)
    norming = 1.0 / math.sqrt(window)
    cosines = jnp.cos(angles) * norming
    sines = jnp.sin(angles) * norming
    forward_fourier = jnp.stack([jnp.stack([cosines, -sines]), jnp.stack([sines, cosines])])
    inverse_fourier = jnp.stack([jnp.stack([cosines, sines]), jnp.stack([-sines, cosines])])
    return (forward_fourier.astype(jnp.bfloat16), inverse_fourier.astype(jnp.bfloat16))


def times(left_value, right_value):
    real_part = (
        left_value[..., 0, :, :] * right_value[..., 0, :, :]
        - left_value[..., 1, :, :] * right_value[..., 1, :, :]
    )
    imag_part = (
        left_value[..., 0, :, :] * right_value[..., 1, :, :]
        + left_value[..., 1, :, :] * right_value[..., 0, :, :]
    )
    return jnp.stack([real_part, imag_part], -3)


def times_conj(left_value, right_value):
    real_part = (
        left_value[..., 0, :, :] * right_value[..., 0, :, :]
        + left_value[..., 1, :, :] * right_value[..., 1, :, :]
    )
    imag_part = (
        left_value[..., 0, :, :] * right_value[..., 1, :, :]
        - left_value[..., 1, :, :] * right_value[..., 0, :, :]
    )
    return jnp.stack([real_part, imag_part], -3)


def refine_object(exit_waves, measured_intensity, forward_fourier, inverse_fourier):
    half_done = jnp.einsum(
        "bcrk,cdkm->bdrm", exit_waves, forward_fourier, preferred_element_type=jnp.float32
    ).astype(jnp.bfloat16)
    spectrum = jnp.einsum(
        "cdrs,bcsm->bdrm", forward_fourier, half_done, preferred_element_type=jnp.float32
    )
    modulus = jnp.sqrt(spectrum[:, 0] * spectrum[:, 0] + spectrum[:, 1] * spectrum[:, 1])
    rescale = measured_intensity.astype(jnp.float32) / jnp.maximum(modulus, 0.5)
    projected = (spectrum * rescale[:, None]).astype(jnp.bfloat16)
    half_back = jnp.einsum(
        "bcrk,cdkm->bdrm", projected, inverse_fourier, preferred_element_type=jnp.float32
    ).astype(jnp.bfloat16)
    returned = jnp.einsum(
        "cdrs,bcsm->bdrm", inverse_fourier, half_back, preferred_element_type=jnp.float32
    )
    return returned - exit_waves.astype(jnp.float32)


def refine_all(exit_waves, measured_intensity, update_marks, forward_fourier, inverse_fourier):
    group_size = BLOCK
    turns = exit_waves.shape[0] // group_size
    collected = jnp.zeros(exit_waves.shape, jnp.float32)

    def advance(position, collected):
        offset = position * group_size
        exit_wave_portion = lax.dynamic_slice_in_dim(exit_waves, offset, group_size, 0)
        measured_part = lax.dynamic_slice_in_dim(measured_intensity, offset, group_size, 0)
        any_used = jnp.any(lax.dynamic_slice_in_dim(update_marks, offset, group_size, 0))
        object_delta = lax.cond(
            any_used,
            lambda exit_wave_current, measurement_current: refine_object(
                exit_wave_current, measurement_current, forward_fourier, inverse_fourier
            ),
            lambda exit_wave_current, measurement_current: jnp.zeros(
                exit_wave_current.shape, jnp.float32
            ),
            exit_wave_portion,
            measured_part,
        )
        return lax.dynamic_update_slice_in_dim(collected, object_delta, offset, 0)

    return lax.fori_loop(0, turns, advance, collected)


def extend(current, window):
    right_rim = from_behind(current[:, :, :window], "col", -1)
    lower_rim = from_behind(current[:, :window, :], "row", -1)
    corner_rim = from_behind(
        current[:, :window, :window], ("row", "col"), -(lax.axis_size("col") + 1)
    )
    widened = jnp.concatenate([current, right_rim], 2)
    lower_wide = jnp.concatenate([lower_rim, corner_rim], 2)
    return jnp.concatenate([widened, lower_wide], 1)


def fold(deposit, window):
    tile_size = deposit.shape[1] - window
    spilled = from_behind(deposit[:, tile_size:, :tile_size], "row", 1)
    right_part = from_behind(deposit[:, :tile_size, tile_size:], "col", 1)
    corner_part = from_behind(
        deposit[:, tile_size:, tile_size:], ("row", "col"), lax.axis_size("col") + 1
    )
    result = deposit[:, :tile_size, :tile_size]
    result = result.at[:, :window, :].add(spilled)
    result = result.at[:, :, :window].add(right_part)
    return result.at[:, :window, :window].add(corner_part)


def sweep(
    current,
    probe,
    work_measured,
    used,
    work_used,
    corner_list,
    forward_fourier,
    inverse_fourier,
    with_light,
):
    window = probe.shape[1]
    tile_size = current.shape[1]
    slots = used.shape[0]
    extended = extend(current, window)
    zero_index = jnp.zeros((), jnp.int32)

    def cut_patch(spot):
        return lax.dynamic_slice(extended, (zero_index, spot[0], spot[1]), (2, window, window))

    patches = jax.vmap(cut_patch)(corner_list)
    exit_waves = times(probe[None], patches).astype(jnp.bfloat16)
    object_delta = refine_all(
        exit_waves, work_measured, work_used, forward_fourier, inverse_fourier
    )
    weights = used.astype(jnp.float32)
    object_delta = object_delta * weights[:, None, None, None]
    pushed = times_conj(probe[None], object_delta)
    if with_light:
        power = probe[0] * probe[0] + probe[1] * probe[1]
        lighting = power[None] * weights[:, None, None]
        pushed = jnp.concatenate([pushed, lighting[:, None]], 1)
    channels = pushed.shape[1]
    deposit = jnp.zeros((channels, tile_size + window, tile_size + window), jnp.float32)

    def place(position, deposit):
        spot = corner_list[position]
        anchor = (zero_index, spot[0], spot[1])
        present = lax.dynamic_slice(deposit, anchor, (channels, window, window))
        return lax.dynamic_update_slice(deposit, present + pushed[position], anchor)

    deposit = lax.fori_loop(0, slots, place, deposit)
    gathered = fold(deposit, window)
    gradient = None
    if not with_light:
        gradient = jnp.sum(times_conj(patches, object_delta), 0)
    return (gathered, gradient)


def on_device(object_field, probe, amplitude, corners, live_count):
    slots = amplitude.shape[2]
    window = probe.shape[1]
    measured_intensity = amplitude.reshape(slots, window, window)
    corner_list = jnp.transpose(corners.reshape(2, slots))
    used = jnp.arange(slots, dtype=jnp.int32) < live_count.reshape(())
    forward_fourier, inverse_fourier = dft_tables(window)
    first_pass, unused_grad = sweep(
        object_field,
        probe,
        measured_intensity,
        used,
        used,
        corner_list,
        forward_fourier,
        inverse_fourier,
        True,
    )
    denominator = first_pass[2] + 4.0
    updated = object_field + first_pass[:2] / denominator
    second_pass, gradient = sweep(
        updated,
        probe,
        measured_intensity,
        used,
        used,
        corner_list,
        forward_fourier,
        inverse_fourier,
        False,
    )
    refined_object = updated + second_pass / denominator
    summed = lax.psum(gradient, ("row", "col"))
    spread = jnp.sqrt(jnp.mean(summed[0] * summed[0] + summed[1] * summed[1]) + 1e-06)
    new_probe = probe + summed / spread
    return (refined_object, new_probe)


def solution(mesh):
    in_specs = (
        P(None, "row", "col"),
        P(),
        P("row", "col", None, None, None),
        P(None, "row", "col", None),
        P("row", "col"),
    )
    out_specs = (P(None, "row", "col"), P())
    return jax.shard_map(
        on_device, mesh=mesh, in_specs=in_specs, out_specs=out_specs, check_vma=False
    )
```

profile of v0, /device:TPU:0, one launch (start us, length us, event | category | flops | bytes accessed | tf_op | source)
XLA Modules:
  0.0 494.4 jit_solution(5692409708058126604)
XLA Ops:
  23.1 49.5 %while.64 = (s32[]{:T(128)}, f32[2,384,384]{2,1,0:T(8,128)}, s32[16,3]{0,1:T(4,128)S(1)}, f32[16,2,128,128]{3,2,1,0:T(8,128)S(1)}, s32[]{:T(128)}) while((s32[]{:T(128)}, f32[2,384,384]{2,1,0:T(8,128)}, s32[16,3]{0,1:T(4,128)S(1)}, f32[16,2,128,128]{3,2,1,0:T(8,128)S(1)}, s32[]{:T(128)}) %tuple.206), condition=%wide.while_cond.6, body=%wide.while_body.6.sunk | while | flops 2 | bytes 262261 | solution.py:140
  23.8 2.4 bitcast_dynamic-update-slice_fusion.4
  26.9 2.4 bitcast_dynamic-update-slice_fusion.4
  30.0 2.4 bitcast_dynamic-update-slice_fusion.4
  33.1 2.4 bitcast_dynamic-update-slice_fusion.4
  36.2 2.4 bitcast_dynamic-update-slice_fusion.4
  39.3 2.4 bitcast_dynamic-update-slice_fusion.4
  42.4 2.4 bitcast_dynamic-update-slice_fusion.4
  45.5 2.4 bitcast_dynamic-update-slice_fusion.4
  48.6 2.4 bitcast_dynamic-update-slice_fusion.4
  51.7 2.4 bitcast_dynamic-update-slice_fusion.4
  54.8 2.4 bitcast_dynamic-update-slice_fusion.4
  57.9 2.4 bitcast_dynamic-update-slice_fusion.4
  60.9 2.4 bitcast_dynamic-update-slice_fusion.4
  64.0 2.4 bitcast_dynamic-update-slice_fusion.4
  67.1 2.4 bitcast_dynamic-update-slice_fusion.4
  70.2 2.4 bitcast_dynamic-update-slice_fusion.4
  75.3 11.3 %while.60 = (s32[]{:T(128)}, f32[16,2,128,128]{3,2,1,0:T(8,128)}, pred[16]{0:T(512)(128)(4,1)S(1)}, bf16[16,2,128,128]{2,3,1,0:T(8,128)(2,1)S(1)}, bf16[2,2,128,...) while((s32[]{:T(128)}, f32[16,2,128,128]{3,2,1,0:T(8,128)}, ...), condition=%wide.region_4.5_spmd, body=%wide.region_0.4_spmd.sunk | while | flops 269615104 | bytes 5898981 | solution.py:95
  91.9 138.5 %while.61 = (s32[]{:T(128)}, f32[3,384,384]{2,1,0:T(8,128)S(1)}, s32[16,2]{0,1:T(2,128)S(1)}, f32[16,3,128,128]{3,2,1,0:T(8,128)}, s32[]{:T(128)}, /*index=5*/s32[]{:T(128)}, s32[]{:T(128)}) while((s32[]{:T(128)}, f32[3,384,384]{2,1,0:T(8,128)S(1)}, s32[16,2]{0,1:T(2,128)S(1)}, f32[16,3,128,128]{3,2,1,0:T(8,128)}, s32[]{:T(128)}, ...), condition=%wide.region_6.7_spmd, body=%wide.region_5.6_spmd.sunk | while | flops 49160 | bytes 983237 | solution.py:163
  97.6 2.7 dynamic_update_slice.35
  106.0 3.0 dynamic_update_slice.35
  114.6 3.1 dynamic_update_slice.35
  123.4 3.1 dynamic_update_slice.35
  132.1 3.1 dynamic_update_slice.35
  140.9 3.1 dynamic_update_slice.35
  149.6 3.0 dynamic_update_slice.35
  158.3 3.1 dynamic_update_slice.35
  167.0 3.1 dynamic_update_slice.35
  175.8 3.0 dynamic_update_slice.35
  184.4 2.9 dynamic_update_slice.35
  193.0 2.7 dynamic_update_slice.35
  201.4 2.8 dynamic_update_slice.35
  209.9 3.1 dynamic_update_slice.35
  218.6 3.1 dynamic_update_slice.35
  227.4 3.0 dynamic_update_slice.35
  230.4 6.3 %collective-permute-start.3 = (f32[3,128,256]{2,1,0:T(8,128)S(1)}, f32[3,128,256]{2,1,0:T(8,128)S(1)}, u32[]{:S(2)}, u32[]{:S(2)}) collective-permute-start(f32[3,128,256]{2,1,0:T(8,128)S(1)} %slice.359), channel_id=1, source_target_pairs={{0,8},{8,16},{16,24},{1,9},{9,17},{17,25},{2,10},{10,18},{18,26},{... | collective-permute-start | bytes 1179656 | tf_op jit(solution)/shard_map/ppermute | solution.py:14
  236.8 4.1 collective-permute-start.4
  241.0 2.7 collective-permute-start.5
  243.8 6.3 %collective-permute-done.4 = f32[3,256,128]{2,1,0:T(8,128)S(1)} collective-permute-done((f32[3,256,128]{2,1,0:T(8,128)S(1)}, f32[3,256,128]{2,1,0:T(8,128)S(1)}, u32[]{:S(2)}, u32[]{:S(2)}) %collective-permute-start.4) | collective-permute-done | bytes 393248 | tf_op jit(solution)/shard_map/ppermute | solution.py:14
  256.6 8.2 %collective-permute-done.8 = f32[2,128,128]{2,1,0:T(8,128)S(1)} collective-permute-done((f32[2,128,128]{2,1,0:T(8,128)S(1)}, f32[2,128,128]{2,1,0:T(8,128)S(1)}, u32[]{:S(2)}, u32[]{:S(2)}) %collective-permute-start.8) | collective-permute-done | bytes 131104 | tf_op jit(solution)/shard_map/ppermute | solution.py:14
  266.1 49.1 %while.65 = (s32[]{:T(128)}, f32[2,384,384]{2,1,0:T(8,128)}, s32[16,3]{0,1:T(4,128)S(1)}, f32[16,2,128,128]{3,2,1,0:T(8,128)S(1)}, s32[]{:T(128)}) while((s32[]{:T(128)}, f32[2,384,384]{2,1,0:T(8,128)}, s32[16,3]{0,1:T(4,128)S(1)}, f32[16,2,128,128]{3,2,1,0:T(8,128)S(1)}, s32[]{:T(128)}) %tuple.235), condition=%wide.while_cond.7, body=%wide.while_body.7.sunk | while | flops 2 | bytes 262261 | solution.py:140
  266.8 2.4 bitcast_dynamic-update-slice_fusion.5
  272.9 2.4 bitcast_dynamic-update-slice_fusion.5
  276.0 2.4 bitcast_dynamic-update-slice_fusion.5
  279.1 2.4 bitcast_dynamic-update-slice_fusion.5
  282.1 2.4 bitcast_dynamic-update-slice_fusion.5
  288.3 2.4 bitcast_dynamic-update-slice_fusion.5
  320.7 11.7 %while.62 = (s32[]{:T(128)}, f32[16,2,128,128]{3,2,1,0:T(8,128)}, pred[16]{0:T(512)(128)(4,1)S(1)}, bf16[16,2,128,128]{2,3,1,0:T(8,128)(2,1)S(1)}, bf16[2,2,128,...) while((s32[]{:T(128)}, f32[16,2,128,128]{3,2,1,0:T(8,128)}, ...), condition=%wide.region_11.12_spmd, body=%wide.region_7.11_spmd.sunk | while | flops 269615104 | bytes 5898981 | solution.py:95
  337.8 126.6 %while.63 = (s32[]{:T(128)}, f32[2,384,384]{2,1,0:T(8,128)S(1)}, s32[16,2]{0,1:T(2,128)S(1)}, f32[16,2,128,128]{3,2,1,0:T(8,128)}, s32[]{:T(128)}, /*index=5*/s32[]{:T(128)}, s32[]{:T(128)}) while((s32[]{:T(128)}, f32[2,384,384]{2,1,0:T(8,128)S(1)}, s32[16,2]{0,1:T(2,128)S(1)}, f32[16,2,128,128]{3,2,1,0:T(8,128)}, s32[]{:T(128)}, ...), condition=%wide.region_13.14_spmd, body=%wide.region_12.13_spmd.sunk | while | flops 32776 | bytes 655557 | solution.py:163
  351.0 2.4 dynamic_update_slice.37
  358.9 2.5 dynamic_update_slice.37
  366.9 2.5 dynamic_update_slice.37
  374.9 2.5 dynamic_update_slice.37
  382.9 2.5 dynamic_update_slice.37
  390.9 2.4 dynamic_update_slice.37
  398.8 2.5 dynamic_update_slice.37
  406.8 2.5 dynamic_update_slice.37
  414.8 2.4 dynamic_update_slice.37
  445.9 2.5 dynamic_update_slice.37
  453.9 2.5 dynamic_update_slice.37
  461.9 2.5 dynamic_update_slice.37
  465.2 9.2 %collective-permute-start.9 = (f32[2,128,256]{2,1,0:T(8,128)}, f32[2,128,256]{2,1,0:T(8,128)S(1)}, u32[]{:S(2)}, u32[]{:S(2)}) collective-permute-start(f32[2,128,256]{2,1,0:T(8,128)} %slice.375), channel_id=1, source_target_pairs={{0,8},{8,16},{16,24},{1,9},{9,17},{17,25},{2,10},{10,18},{18,26},{... | collective-permute-start | bytes 786440 | tf_op jit(solution)/shard_map/ppermute | solution.py:14
  474.5 3.7 collective-permute-start.10
  478.2 3.6 collective-permute-start.11
  (317 shorter events, 176.6 us)
Async XLA Ops:
  7.2 12.0 %copy-start.8 = (bf16[1,1,16,128,128]{4,3,2,1,0:T(8,128)(2,1)S(1)}, bf16[1,1,16,128,128]{4,3,2,1,0:T(8,128)(2,1)}, u32[]{:S(2)}) copy-start(bf16[1,1,16,128,128]{4,3,2,1,0:T(8,128)(2,1)} %param.31) | copy-start | bytes 1572868
  7.2 474.6 %all-reduce.2.cloned.1.call-start = ((), (), s32[]{:S(2)}) async-start(), calls=%async_computation | async-start | bytes 262144 | tf_op jit(solution)/shard_map/psum | solution.py:203
  8.2 13.6 %collective-permute-start = (f32[2,256,128]{2,1,0:T(8,128)S(1)}, f32[2,256,128]{2,1,0:T(8,128)S(1)}, u32[]{:S(2)}, u32[]{:S(2)}) collective-permute-start(f32[2,256,128]{2,1,0:T(8,128)S(1)} %slice.345), channel_id=1, source_target_pairs={{1,0},{2,1},{3,2},{4,3},{5,4},{6,5},{7,6},{9,8},{10,9},{11,10},{12... | collective-permute-start | bytes 786440 | tf_op jit(solution)/shard_map/ppermute | solution.py:14
  10.5 11.3 %copy-start.4 = (f32[2,256,256]{2,1,0:T(8,128)S(1)}, f32[2,256,256]{2,1,0:T(8,128)}, u32[]{:S(2)}) copy-start(f32[2,256,256]{2,1,0:T(8,128)} %param.29) | copy-start | bytes 1572868
  10.5 11.3 %collective-permute-start.1 = (f32[2,128,256]{2,1,0:T(8,128)S(1)}, f32[2,128,256]{2,1,0:T(8,128)S(1)}, u32[]{:S(2)}, u32[]{:S(2)}) collective-permute-start(f32[2,128,256]{2,1,0:T(8,128)S(1)} %slice.346), channel_id=1, source_target_pairs={{8,0},{16,8},{24,16},{9,1},{17,9},{25,17},{10,2},{18,10},{26,18},{... | collective-permute-start | bytes 786440 | tf_op jit(solution)/shard_map/ppermute | solution.py:14
  12.9 8.9 %collective-permute-start.2 = (f32[2,128,128]{2,1,0:T(8,128)S(1)}, f32[2,128,128]{2,1,0:T(8,128)S(1)}, u32[]{:S(2)}, u32[]{:S(2)}) collective-permute-start(f32[2,128,128]{2,1,0:T(8,128)S(1)} %slice.347), channel_id=1, source_target_pairs={{9,0},{10,1},{11,2},{12,3},{13,4},{14,5},{15,6},{16,7},{17,8},{18,... | collective-permute-start | bytes 393224 | tf_op jit(solution)/shard_map/ppermute | solution.py:14
  86.6 2.1 copy-start.3
  88.7 1.2 copy-start.6
  89.9 2.0 copy-start.9
  230.4 13.3 %collective-permute-start.3 = (f32[3,128,256]{2,1,0:T(8,128)S(1)}, f32[3,128,256]{2,1,0:T(8,128)S(1)}, u32[]{:S(2)}, u32[]{:S(2)}) collective-permute-start(f32[3,128,256]{2,1,0:T(8,128)S(1)} %slice.359), channel_id=1, source_target_pairs={{0,8},{8,16},{16,24},{1,9},{9,17},{17,25},{2,10},{10,18},{18,26},{... | collective-permute-start | bytes 1179656 | tf_op jit(solution)/shard_map/ppermute | solution.py:14
  236.8 13.3 %collective-permute-start.4 = (f32[3,256,128]{2,1,0:T(8,128)S(1)}, f32[3,256,128]{2,1,0:T(8,128)S(1)}, u32[]{:S(2)}, u32[]{:S(2)}) collective-permute-start(f32[3,256,128]{2,1,0:T(8,128)S(1)} %slice.361), channel_id=1, source_target_pairs={{0,1},{1,2},{2,3},{3,4},{4,5},{5,6},{6,7},{8,9},{9,10},{10,11},{11... | collective-permute-start | bytes 1179656 | tf_op jit(solution)/shard_map/ppermute | solution.py:14
  241.0 11.6 %copy-start.5 = (f32[2,256,256]{2,1,0:T(8,128)S(1)}, f32[2,256,256]{2,1,0:T(8,128)}, u32[]{:S(2)}) copy-start(f32[2,256,256]{2,1,0:T(8,128)} %param.29) | copy-start | bytes 1572868
  241.0 11.5 %collective-permute-start.5 = (f32[3,128,128]{2,1,0:T(8,128)S(1)}, f32[3,128,128]{2,1,0:T(8,128)S(1)}, u32[]{:S(2)}, u32[]{:S(2)}) collective-permute-start(f32[3,128,128]{2,1,0:T(8,128)S(1)} %slice.363), channel_id=1, source_target_pairs={{0,9},{1,10},{2,11},{3,12},{4,13},{5,14},{6,15},{7,16},{8,17},{9,1... | collective-permute-start | bytes 589832 | tf_op jit(solution)/shard_map/ppermute | solution.py:14
  252.7 12.1 %collective-permute-start.6 = (f32[2,256,128]{2,1,0:T(8,128)S(1)}, f32[2,256,128]{2,1,0:T(8,128)S(1)}, u32[]{:S(2)}, u32[]{:S(2)}) collective-permute-start(f32[2,256,128]{2,1,0:T(8,128)S(1)} %slice.424), channel_id=1, source_target_pairs={{1,0},{2,1},{3,2},{4,3},{5,4},{6,5},{7,6},{9,8},{10,9},{11,10},{12... | collective-permute-start | bytes 786440 | tf_op jit(solution)/shard_map/ppermute | solution.py:14
  254.0 10.8 %collective-permute-start.7 = (f32[2,128,256]{2,1,0:T(8,128)S(1)}, f32[2,128,256]{2,1,0:T(8,128)S(1)}, u32[]{:S(2)}, u32[]{:S(2)}) collective-permute-start(f32[2,128,256]{2,1,0:T(8,128)S(1)} %slice.425), channel_id=1, source_target_pairs={{8,0},{16,8},{24,16},{9,1},{17,9},{25,17},{10,2},{18,10},{26,18},{... | collective-permute-start | bytes 786440 | tf_op jit(solution)/shard_map/ppermute | solution.py:14
  255.3 9.5 %collective-permute-start.8 = (f32[2,128,128]{2,1,0:T(8,128)S(1)}, f32[2,128,128]{2,1,0:T(8,128)S(1)}, u32[]{:S(2)}, u32[]{:S(2)}) collective-permute-start(f32[2,128,128]{2,1,0:T(8,128)S(1)} %slice.426), channel_id=1, source_target_pairs={{9,0},{10,1},{11,2},{12,3},{13,4},{14,5},{15,6},{16,7},{17,8},{18,... | collective-permute-start | bytes 393224 | tf_op jit(solution)/shard_map/ppermute | solution.py:14
  315.2 1.6 copy-start
  319.1 1.6 copy-start.2
  332.4 2.2 copy-start.1
  464.4 19.5 %copy-start.7 = (f32[2,128,128]{2,1,0:T(8,128)S(1)}, f32[2,128,128]{2,1,0:T(8,128)}, u32[]{:S(2)}) copy-start(f32[2,128,128]{2,1,0:T(8,128)} %param.30) | copy-start | bytes 393220
  465.2 20.3 %collective-permute-start.9 = (f32[2,128,256]{2,1,0:T(8,128)}, f32[2,128,256]{2,1,0:T(8,128)S(1)}, u32[]{:S(2)}, u32[]{:S(2)}) collective-permute-start(f32[2,128,256]{2,1,0:T(8,128)} %slice.375), channel_id=1, source_target_pairs={{0,8},{8,16},{16,24},{1,9},{9,17},{17,25},{2,10},{10,18},{18,26},{... | collective-permute-start | bytes 786440 | tf_op jit(solution)/shard_map/ppermute | solution.py:14
  474.5 11.1 %collective-permute-start.10 = (f32[2,256,128]{2,1,0:T(8,128)S(1)}, f32[2,256,128]{2,1,0:T(8,128)}, u32[]{:S(2)}, u32[]{:S(2)}) collective-permute-start(f32[2,256,128]{2,1,0:T(8,128)S(1)} %slice.377), channel_id=1, source_target_pairs={{0,1},{1,2},{2,3},{3,4},{4,5},{5,6},{6,7},{8,9},{9,10},{10,11},{11... | collective-permute-start | bytes 786440 | tf_op jit(solution)/shard_map/ppermute | solution.py:14
  478.2 8.5 %collective-permute-start.11 = (f32[2,128,128]{2,1,0:T(8,128)S(1)}, f32[2,128,128]{2,1,0:T(8,128)S(1)}, u32[]{:S(2)}, u32[]{:S(2)}) collective-permute-start(f32[2,128,128]{2,1,0:T(8,128)S(1)} %slice.379), channel_id=1, source_target_pairs={{0,9},{1,10},{2,11},{3,12},{4,13},{5,14},{6,15},{7,16},{8,17},{9,1... | collective-permute-start | bytes 393224 | tf_op jit(solution)/shard_map/ppermute | solution.py:14
Sparse Core Ops, SparseCore 0:
  336.4 132.6 all-reduce.1
where the time goes:
time: 502 us; the launch traced here: 494 us
  local copies, waits for them, and re-layouts  226 us (45%)
  loops' own time  131 us (26%)
  other arithmetic  62.6 us (12%)
  starting transfers between devices  37.5 us (7%)
  waiting for transfers between devices  19 us (4%)
  between operations  15.9 us (3%)
    another operation x2, loops' own time, sweep(): deposit = lax.fori_loop(0, slots, place, deposit)  125 us
    gather x96, local copies, waits for them, and re-layouts  98 us
    dynamic_update_slice x32, local copies, waits for them, and re-layouts, place(): return lax.dynamic_update_slice(deposit, present + pushed[position], anchor)  85.9 us
    ppermute x12, starting transfers between devices, from_behind(): lax.ppermute(value, axis, [(source, source + steps) for source in range(f...  37.5 us
    add x32, other arithmetic, place(): return lax.dynamic_update_slice(deposit, present + pushed[position], anchor)  33.2 us
    ppermute x12, waiting for transfers between devices, from_behind(): lax.ppermute(value, axis, [(source, source + steps) for source in range(f...  19 us
    slice x32, local copies, waits for them, and re-layouts, place(): anchor = (zero_index, spot[0], spot[1])  18.3 us
  transfers between devices with their start and end apart: 13, of which 4 were waited for; matrix products, arithmetic and copies ran while one was open for 16% of the time, Pallas kernels for 0%

commit v1 on v0

v1 whole, which is shorter than its diff:
```python
import functools
import math

import jax
import jax.numpy as jnp
import numpy as np
from jax import lax
from jax.experimental import pallas as pl
from jax.experimental.pallas import tpu as pltpu
from jax.sharding import PartitionSpec as P

GROUP = 4


def from_behind(value, axis, steps):
    count = lax.axis_size(axis)
    first, last = (max(0, -steps), min(count, count - steps))
    return lax.ppermute(value, axis, [(source, source + steps) for source in range(first, last)])


def dft_tables(window):
    indices = np.arange(window, dtype=np.int32)
    phase_index = indices[:, None] * indices[None, :] % window
    angles = phase_index.astype(np.float32) * np.float32(2.0 * math.pi / window)
    norming = np.float32(1.0 / math.sqrt(window))
    cosines = np.cos(angles) * norming
    sines = np.sin(angles) * norming
    forward = np.block([[cosines, -sines], [sines, cosines]]).astype(np.float32)
    return (jnp.asarray(forward, jnp.bfloat16), jnp.asarray(forward.T.copy(), jnp.bfloat16))


def dot(left, right):
    return jnp.dot(left, right, preferred_element_type=jnp.float32)


def sweep_kernel(with_light, corners, live, ext, probe, amp, ahead, back, deposit, *rest):
    if with_light:
        waves_buf = rest[0]
    else:
        gradient, waves_buf, patch_buf = rest
        gradient[...] = jnp.zeros_like(gradient)
    slots, win = amp.shape[0], amp.shape[1]
    deposit[...] = jnp.zeros_like(deposit)
    lane = lax.broadcasted_iota(jnp.int32, (win, win), 1)
    used = live[0]

    def spot(slot):
        row, col = corners[0, slot], corners[1, slot]
        base = col // win
        return row, base, col - base * win

    def add_at(plane, row, base, shift, value):
        turned = pltpu.roll(value, shift, 1)
        left = jnp.where(lane >= shift, turned, 0.0)
        right = jnp.where(lane >= shift, 0.0, turned)
        for offset, part in ((0, left), (1, right)):
            at = (plane, base + offset, pl.ds(row, win))
            deposit[at] = deposit[at] + part

    @pl.loop(0, (used + GROUP - 1) // GROUP)
    def _(turn):
        first = turn * GROUP
        pr, pi = probe[0], probe[1]
        for member in range(GROUP):
            row, base, shift = spot(first + member)
            parts = []
            for plane in range(2):
                left = ext[plane, base, pl.ds(row, win)]
                right = ext[plane, base + 1, pl.ds(row, win)]
                mixed = jnp.where(lane >= shift, left, right)
                parts.append(pltpu.roll(mixed, lax.rem(win - shift, win), 1))
            re, im = parts
            if not with_light:
                patch_buf[member, 0] = re
                patch_buf[member, 1] = im
            rows = pl.ds(member * win, win)
            waves_buf[rows, :win] = (pr * re - pi * im).astype(jnp.bfloat16)
            waves_buf[rows, win:] = (pr * im + pi * re).astype(jnp.bfloat16)
        half = dot(waves_buf[...], ahead[...]).astype(jnp.bfloat16)

        def upright(value):
            columns = []
            for member in range(GROUP):
                block = value[member * win : (member + 1) * win]
                columns.append(jnp.concatenate([block[:, :win], block[:, win:]], 0))
            return jnp.concatenate(columns, 1)

        spectrum = dot(back[...], upright(half))
        projected = []
        for member in range(GROUP):
            re = spectrum[:win, member * win : (member + 1) * win]
            im = spectrum[win:, member * win : (member + 1) * win]
            scale = amp[first + member].astype(jnp.float32) * lax.rsqrt(
                jnp.maximum(re * re + im * im, 0.25)
            )
            projected.append(
                jnp.concatenate(
                    [(re * scale).astype(jnp.bfloat16), (im * scale).astype(jnp.bfloat16)], 1
                )
            )
        half_back = dot(jnp.concatenate(projected, 0), back[...]).astype(jnp.bfloat16)
        returned = dot(ahead[...], upright(half_back))
        for member in range(GROUP):
            slot = first + member
            weight = jnp.where(slot < used, 1.0, 0.0)
            row, base, shift = spot(slot)
            rows = pl.ds(member * win, win)
            columns = slice(member * win, (member + 1) * win)
            re = (returned[:win, columns] - waves_buf[rows, :win].astype(jnp.float32)) * weight
            im = (returned[win:, columns] - waves_buf[rows, win:].astype(jnp.float32)) * weight
            add_at(0, row, base, shift, pr * re + pi * im)
            add_at(1, row, base, shift, pr * im - pi * re)
            if with_light:
                add_at(2, row, base, shift, (pr * pr + pi * pi) * weight)
            else:
                ore, oim = patch_buf[member, 0], patch_buf[member, 1]
                gradient[0] += ore * re + oim * im
                gradient[1] += ore * im - oim * re


def sweep(with_light, corners, live, ext, probe, amp, ahead, back):
    slots, win = amp.shape[0], amp.shape[1]
    strips, side = ext.shape[1:3]
    vmem = pl.BlockSpec(memory_space=pltpu.VMEM)
    smem = pl.BlockSpec(memory_space=pltpu.SMEM)
    planes = 3 if with_light else 2
    out_shape = [jax.ShapeDtypeStruct((planes, strips, side, win), jnp.float32)]
    scratch = [pltpu.VMEM((GROUP * win, 2 * win), jnp.bfloat16)]
    if not with_light:
        out_shape.append(jax.ShapeDtypeStruct((2, win, win), jnp.float32))
        scratch.append(pltpu.VMEM((GROUP, 2, win, win), jnp.float32))
    return pl.pallas_call(
        functools.partial(sweep_kernel, with_light),
        out_shape=out_shape,
        in_specs=[smem, smem] + [vmem] * 5,
        out_specs=[vmem] * len(out_shape),
        scratch_shapes=scratch,
        name="first_sweep" if with_light else "second_sweep",
    )(corners, live, ext, probe, amp, ahead, back)


def strips_of(value, window):
    planes, rows, columns = value.shape
    return jnp.transpose(value.reshape(planes, rows, columns // window, window), (0, 2, 1, 3))


def extend(current, window):
    right_rim = from_behind(current[:, :, :window], "col", -1)
    lower_rim = from_behind(current[:, :window, :], "row", -1)
    corner_rim = from_behind(
        current[:, :window, :window], ("row", "col"), -(lax.axis_size("col") + 1)
    )
    widened = jnp.concatenate([current, right_rim], 2)
    lower_wide = jnp.concatenate([lower_rim, corner_rim], 2)
    return strips_of(jnp.concatenate([widened, lower_wide], 1), window)


def fold(deposit, window):
    deposit = jnp.transpose(deposit, (0, 2, 1, 3)).reshape(deposit.shape[0], deposit.shape[2], -1)
    tile_size = deposit.shape[1] - window
    spilled = from_behind(deposit[:, tile_size:, :tile_size], "row", 1)
    right_part = from_behind(deposit[:, :tile_size, tile_size:], "col", 1)
    corner_part = from_behind(
        deposit[:, tile_size:, tile_size:], ("row", "col"), lax.axis_size("col") + 1
    )
    result = deposit[:, :tile_size, :tile_size]
    result = result.at[:, :window, :].add(spilled)
    result = result.at[:, :, :window].add(right_part)
    return result.at[:, :window, :window].add(corner_part)


def on_device(object_field, probe, amplitude, corners, live_count):
    slots = amplitude.shape[2]
    window = probe.shape[1]
    amp = amplitude.reshape(slots, window, window)
    corners = corners.reshape(2, slots)
    live = live_count.reshape(1)
    ahead, back = dft_tables(window)
    (deposit,) = sweep(True, corners, live, extend(object_field, window), probe, amp, ahead, back)
    first_pass = fold(deposit, window)
    denominator = first_pass[2] + 4.0
    updated = object_field + first_pass[:2] / denominator
    deposit, gradient = sweep(
        False, corners, live, extend(updated, window), probe, amp, ahead, back
    )
    refined_object = updated + fold(deposit, window) / denominator
    summed = lax.psum(gradient, ("row", "col"))
    spread = jnp.sqrt(jnp.mean(summed[0] * summed[0] + summed[1] * summed[1]) + 1e-06)
    new_probe = probe + summed / spread
    return (refined_object, new_probe)


def solution(mesh):
    in_specs = (
        P(None, "row", "col"),
        P(),
        P("row", "col", None, None, None),
        P(None, "row", "col", None),
        P("row", "col"),
    )
    out_specs = (P(None, "row", "col"), P())
    return jax.shard_map(
        on_device, mesh=mesh, in_specs=in_specs, out_specs=out_specs, check_vma=False
    )
```

time: 502 us -> 214 us (0.43); the launches traced: 494 us -> 215 us
  local copies, waits for them, and re-layouts: 226 us -> 9.86 us
  loops' own time: 131 us -> 0 us
  waiting for transfers between devices: 19 us -> 140 us
  other arithmetic: 62.6 us -> 4.74 us
  Pallas kernels: 0 us -> 10.2 us
    another operation x14 -> x0, loops' own time: 131 us -> none  [the longest x2 125 us: sweep(): deposit = lax.fori_loop(0, slots, place, deposit)]
    psum x1, waiting for transfers between devices: 0.02 us -> 117 us  [on_device(): summed = lax.psum(gradient, ('row', 'col'))]
    gather x96 -> x0, local copies, waits for them, and re-layouts: 98 us -> none
    dynamic_update_slice x48 -> x0, local copies, waits for them, and re-layouts: 94.2 us -> none  [the longest x32 85.9 us: place(): return lax.dynamic_update_slice(deposit, present + pushed[position], anchor)]
    add x35 -> x1, other arithmetic: 35.2 us -> 0.08 us  [on_device(): refined_object = updated + fold(deposit, window) / denominator]
    slice x32 -> x0, local copies, waits for them, and re-layouts: 18.3 us -> none  [place(): anchor = (zero_index, spot[0], spot[1])]
    pallas_call x0 -> x2, Pallas kernels: none -> 10.2 us  [sweep(): pl.pallas_call(functools.partial(sweep_kernel, with_light), out_shape=out...]
    mul x4 -> x0, other arithmetic: 6.07 us -> none  [the longest x2 4.06 us: sweep(): object_delta = object_delta * weights[:, None, None, None]]
  transfers between devices with their start and end apart: 13 -> 13, of which waited for: 4 -> 5; matrix products, arithmetic and copies ran while one was open for 16% -> 3% of each run, Pallas kernels for 0% -> 0%
where the time goes in v1:
time: 214 us; the launch traced here: 215 us
  waiting for transfers between devices  140 us (65%)
  starting transfers between devices  34 us (16%)
  between operations  15.7 us (7%)
  Pallas kernels  10.2 us (5%)
  local copies, waits for them, and re-layouts  9.86 us (5%)
  other arithmetic  4.74 us (2%)
    psum x1, waiting for transfers between devices, on_device(): summed = lax.psum(gradient, ('row', 'col'))  117 us
    ppermute x12, starting transfers between devices, from_behind(): lax.ppermute(value, axis, [(source, source + steps) for source in range(f...  34 us
    ppermute x12, waiting for transfers between devices, from_behind(): lax.ppermute(value, axis, [(source, source + steps) for source in range(f...  23.2 us
    pallas_call x2, Pallas kernels, sweep(): pl.pallas_call(functools.partial(sweep_kernel, with_light), out_shape=out...  10.2 us
  transfers between devices with their start and end apart: 13, of which 5 were waited for; matrix products, arithmetic and copies ran while one was open for 3% of the time, Pallas kernels for 0%

profile of v1, /device:TPU:0, one launch (start us, length us, event | category | flops | bytes accessed | tf_op | source)
XLA Modules:
  0.0 214.6 jit_solution(2102388010891845776)
XLA Ops:
  7.2 0.0 all-reduce.2.cloned.1.call-start
  7.2 1.2 copy.15
  8.5 1.3 collective-permute-start
  9.8 1.3 collective-permute-start.1
  11.1 1.3 collective-permute-start.2
  13.1 8.0 %collective-permute-done.2 = f32[2,128,128]{1,2,0:T(8,128)S(1)} collective-permute-done((f32[2,128,128]{1,2,0:T(8,128)S(1)}, f32[2,128,128]{1,2,0:T(8,128)S(1)}, u32[]{:S(2)}, u32[]{:S(2)}) %collective-permute-start.2) | collective-permute-done | bytes 131104 | tf_op jit(solution)/shard_map/ppermute | solution.py:18
  21.1 0.0 collective-permute-done
  21.1 0.0 collective-permute-done.1
  21.1 0.1 maximum_maximum_fusion
  21.2 1.4 copy.13
  22.6 5.2 %first_sweep.1 = f32[3,3,384,128]{3,2,1,0:T(8,128)} custom-call(s32[2,16]{1,0:T(2,128)} %bitcast.33, s32[1]{0:T(128)} %bitcast.13.live, f32[2,3,384,128]{3,2,1,0:T(8,128)} %bitcast.26, f32[2,128,128]{2,1,0:T(8,128)} %probe.3, bf16[16,128,128]{2,1,0:T(8,128)(2,1)} %bitcast.30, bf16[256,256]{1,0:T(8,128)(2,1)} %constant.155.clone.ahead, ...), custom_call_target="tpu_custom_call" | custom-call | tf_op jit(solution)/shard_map/first_sweep/pallas_call | solution.py:132
  27.7 2.2 %copy.14 = f32[3,384,3,128]{1,3,2,0:T(8,128)S(1)} copy(f32[3,384,3,128]{3,1,2,0:T(8,128)} %bitcast.20) | data formatting | bytes 3538944 | tf_op jit(solution)/shard_map/transpose | solution.py:159
  30.0 3.2 %collective-permute-start.3 = (f32[3,128,256]{1,2,0:T(8,128)S(1)}, f32[3,128,256]{1,2,0:T(8,128)S(1)}, u32[]{:S(2)}, u32[]{:S(2)}) collective-permute-start(f32[3,128,256]{1,2,0:T(8,128)S(1)} %slice.241), channel_id=1, source_target_pairs={{0,8},{8,16},{16,24},{1,9},{9,17},{17,25},{2,10},{10,18},{18,26},{... | collective-permute-start | bytes 1179656 | tf_op jit(solution)/shard_map/ppermute | solution.py:18
  33.2 5.5 %collective-permute-start.4 = (f32[3,256,128]{1,2,0:T(8,128)S(1)}, f32[3,256,128]{1,2,0:T(8,128)S(1)}, u32[]{:S(2)}, u32[]{:S(2)}) collective-permute-start(f32[3,256,128]{1,2,0:T(8,128)S(1)} %slice.243), channel_id=1, source_target_pairs={{0,1},{1,2},{2,3},{3,4},{4,5},{5,6},{6,7},{8,9},{9,10},{10,11},{11... | collective-permute-start | bytes 1179656 | tf_op jit(solution)/shard_map/ppermute | solution.py:18
  38.7 0.1 slice.239
  38.8 3.9 %collective-permute-start.5 = (f32[3,128,128]{1,2,0:T(8,128)S(1)}, f32[3,128,128]{1,2,0:T(8,128)S(1)}, u32[]{:S(2)}, u32[]{:S(2)}) collective-permute-start(f32[3,128,128]{1,2,0:T(8,128)S(1)} %slice.245), channel_id=1, source_target_pairs={{0,9},{1,10},{2,11},{3,12},{4,13},{5,14},{6,15},{7,16},{8,17},{9,1... | collective-permute-start | bytes 589832 | tf_op jit(solution)/shard_map/ppermute | solution.py:18
  42.7 0.0 collective-permute-done.3
  42.7 0.1 fusion.1
  42.7 4.7 %collective-permute-done.4 = f32[3,256,128]{1,2,0:T(8,128)S(1)} collective-permute-done((f32[3,256,128]{1,2,0:T(8,128)S(1)}, f32[3,256,128]{1,2,0:T(8,128)S(1)}, u32[]{:S(2)}, u32[]{:S(2)}) %collective-permute-start.4) | collective-permute-done | bytes 393248 | tf_op jit(solution)/shard_map/ppermute | solution.py:18
  47.4 0.2 constant_dynamic-update-slice_fusion.1
  47.5 1.9 collective-permute-done.5
  49.5 0.1 fusion
  49.7 1.3 collective-permute-start.6
  51.0 1.3 collective-permute-start.7
  52.3 1.3 collective-permute-start.8
  53.6 8.6 %collective-permute-done.8 = f32[2,128,128]{1,2,0:T(8,128)S(1)} collective-permute-done((f32[2,128,128]{1,2,0:T(8,128)S(1)}, f32[2,128,128]{1,2,0:T(8,128)S(1)}, u32[]{:S(2)}, u32[]{:S(2)}) %collective-permute-start.8) | collective-permute-done | bytes 131104 | tf_op jit(solution)/shard_map/ppermute | solution.py:18
  62.2 0.0 collective-permute-done.6
  62.2 0.0 collective-permute-done.7
  62.2 0.1 maximum_maximum_fusion.1
  62.3 1.4 copy.16
  63.7 5.0 %second_sweep.1 = (f32[2,3,384,128]{3,2,1,0:T(8,128)}, f32[2,128,128]{2,1,0:T(8,128)}) custom-call(s32[2,16]{1,0:T(2,128)} %bitcast.34, s32[1]{0:T(128)} %bitcast.14.live, f32[2,3,384,128]{3,2,1,0:T(8,128)} %bitcast.27, f32[2,128,128]{2,1,0:T(8,128)} %probe.3, bf16[16,128,128]{2,1,0:T(8,128)(2,1)} %bitcast.31, bf16[256,256]{1,0:T(8,128)(2,1)} %constant.155.clone.ahead, ...), custom_call_target="tpu_custom_call" | custom-call | tf_op jit(solution)/shard_map/second_sweep/pallas_call | solution.py:132
  68.6 0.0 all-reduce.2.cloned.1.call-update
  68.7 1.6 copy.17
  70.3 0.0 copy-start
  70.4 0.7 slice.257
  71.1 3.9 %collective-permute-start.9 = (f32[2,128,256]{1,2,0:T(8,128)S(1)}, f32[2,128,256]{1,2,0:T(8,128)S(1)}, u32[]{:S(2)}, u32[]{:S(2)}) collective-permute-start(f32[2,128,256]{1,2,0:T(8,128)S(1)} %slice.253), channel_id=1, source_target_pairs={{0,8},{8,16},{16,24},{1,9},{9,17},{17,25},{2,10},{10,18},{18,26},{... | collective-permute-start | bytes 786440 | tf_op jit(solution)/shard_map/ppermute | solution.py:18
  75.0 6.6 %collective-permute-start.10 = (f32[2,256,128]{1,2,0:T(8,128)S(1)}, f32[2,256,128]{1,2,0:T(8,128)}, u32[]{:S(2)}, u32[]{:S(2)}) collective-permute-start(f32[2,256,128]{1,2,0:T(8,128)S(1)} %slice.255), channel_id=1, source_target_pairs={{0,1},{1,2},{2,3},{3,4},{4,5},{5,6},{6,7},{8,9},{9,10},{10,11},{11... | collective-permute-start | bytes 786440 | tf_op jit(solution)/shard_map/ppermute | solution.py:18
  81.6 3.2 %collective-permute-start.11 = (f32[2,128,128]{1,2,0:T(8,128)}, f32[2,128,128]{1,2,0:T(8,128)S(1)}, u32[]{:S(2)}, u32[]{:S(2)}) collective-permute-start(f32[2,128,128]{1,2,0:T(8,128)} %slice.257), channel_id=1, source_target_pairs={{0,9},{1,10},{2,11},{3,12},{4,13},{5,14},{6,15},{7,16},{8,17},{9,1... | collective-permute-start | bytes 393224 | tf_op jit(solution)/shard_map/ppermute | solution.py:18
  84.8 117.0 %all-reduce.2.cloned.1.call-done = f32[2,128,128]{2,1,0:T(8,128)} async-done(((f32[2,128,128]{2,1,0:T(8,128)}), f32[2,128,128]{2,1,0:T(8,128)}) %all-reduce.2.cloned.1.call-update) | async-done | bytes 131088 | tf_op jit(solution)/shard_map/psum | solution.py:187
  201.8 1.5 fusion.7
  204.0 0.0 copy-done
  204.0 1.6 divide_add_fusion.1
  205.6 0.0 collective-permute-done.9
  205.6 0.0 collective-permute-done.10
  205.6 1.0 constant_dynamic-update-slice_fusion
  206.7 0.0 collective-permute-done.11
  206.7 0.1 divide_add_fusion
  206.8 1.0 copy.18
  (16 shorter events, 0.3 us)
Async XLA Ops:
  7.2 194.6 %all-reduce.2.cloned.1.call-start = ((), (), s32[]{:S(2)}) async-start(), calls=%async_computation | async-start | bytes 262144 | tf_op jit(solution)/shard_map/psum | solution.py:187
  8.5 12.6 %collective-permute-start = (f32[2,256,128]{1,2,0:T(8,128)S(1)}, f32[2,256,128]{1,2,0:T(8,128)S(1)}, u32[]{:S(2)}, u32[]{:S(2)}) collective-permute-start(f32[2,256,128]{1,2,0:T(8,128)S(1)} %slice.236), channel_id=1, source_target_pairs={{1,0},{2,1},{3,2},{4,3},{5,4},{6,5},{7,6},{9,8},{10,9},{11,10},{12... | collective-permute-start | bytes 786440 | tf_op jit(solution)/shard_map/ppermute | solution.py:18
  9.8 11.3 %collective-permute-start.1 = (f32[2,128,256]{1,2,0:T(8,128)S(1)}, f32[2,128,256]{1,2,0:T(8,128)S(1)}, u32[]{:S(2)}, u32[]{:S(2)}) collective-permute-start(f32[2,128,256]{1,2,0:T(8,128)S(1)} %slice.237), channel_id=1, source_target_pairs={{8,0},{16,8},{24,16},{9,1},{17,9},{25,17},{10,2},{18,10},{26,18},{... | collective-permute-start | bytes 786440 | tf_op jit(solution)/shard_map/ppermute | solution.py:18
  11.1 10.0 %collective-permute-start.2 = (f32[2,128,128]{1,2,0:T(8,128)S(1)}, f32[2,128,128]{1,2,0:T(8,128)S(1)}, u32[]{:S(2)}, u32[]{:S(2)}) collective-permute-start(f32[2,128,128]{1,2,0:T(8,128)S(1)} %slice.238), channel_id=1, source_target_pairs={{9,0},{10,1},{11,2},{12,3},{13,4},{14,5},{15,6},{16,7},{17,8},{18,... | collective-permute-start | bytes 393224 | tf_op jit(solution)/shard_map/ppermute | solution.py:18
  30.0 12.7 %collective-permute-start.3 = (f32[3,128,256]{1,2,0:T(8,128)S(1)}, f32[3,128,256]{1,2,0:T(8,128)S(1)}, u32[]{:S(2)}, u32[]{:S(2)}) collective-permute-start(f32[3,128,256]{1,2,0:T(8,128)S(1)} %slice.241), channel_id=1, source_target_pairs={{0,8},{8,16},{16,24},{1,9},{9,17},{17,25},{2,10},{10,18},{18,26},{... | collective-permute-start | bytes 1179656 | tf_op jit(solution)/shard_map/ppermute | solution.py:18
  33.2 14.1 %collective-permute-start.4 = (f32[3,256,128]{1,2,0:T(8,128)S(1)}, f32[3,256,128]{1,2,0:T(8,128)S(1)}, u32[]{:S(2)}, u32[]{:S(2)}) collective-permute-start(f32[3,256,128]{1,2,0:T(8,128)S(1)} %slice.243), channel_id=1, source_target_pairs={{0,1},{1,2},{2,3},{3,4},{4,5},{5,6},{6,7},{8,9},{9,10},{10,11},{11... | collective-permute-start | bytes 1179656 | tf_op jit(solution)/shard_map/ppermute | solution.py:18
  38.8 10.7 %collective-permute-start.5 = (f32[3,128,128]{1,2,0:T(8,128)S(1)}, f32[3,128,128]{1,2,0:T(8,128)S(1)}, u32[]{:S(2)}, u32[]{:S(2)}) collective-permute-start(f32[3,128,128]{1,2,0:T(8,128)S(1)} %slice.245), channel_id=1, source_target_pairs={{0,9},{1,10},{2,11},{3,12},{4,13},{5,14},{6,15},{7,16},{8,17},{9,1... | collective-permute-start | bytes 589832 | tf_op jit(solution)/shard_map/ppermute | solution.py:18
  49.7 12.5 %collective-permute-start.6 = (f32[2,256,128]{1,2,0:T(8,128)S(1)}, f32[2,256,128]{1,2,0:T(8,128)S(1)}, u32[]{:S(2)}, u32[]{:S(2)}) collective-permute-start(f32[2,256,128]{1,2,0:T(8,128)S(1)} %slice.248), channel_id=1, source_target_pairs={{1,0},{2,1},{3,2},{4,3},{5,4},{6,5},{7,6},{9,8},{10,9},{11,10},{12... | collective-permute-start | bytes 786440 | tf_op jit(solution)/shard_map/ppermute | solution.py:18
  51.0 11.2 %collective-permute-start.7 = (f32[2,128,256]{1,2,0:T(8,128)S(1)}, f32[2,128,256]{1,2,0:T(8,128)S(1)}, u32[]{:S(2)}, u32[]{:S(2)}) collective-permute-start(f32[2,128,256]{1,2,0:T(8,128)S(1)} %slice.249), channel_id=1, source_target_pairs={{8,0},{16,8},{24,16},{9,1},{17,9},{25,17},{10,2},{18,10},{26,18},{... | collective-permute-start | bytes 786440 | tf_op jit(solution)/shard_map/ppermute | solution.py:18
  52.3 9.9 %collective-permute-start.8 = (f32[2,128,128]{1,2,0:T(8,128)S(1)}, f32[2,128,128]{1,2,0:T(8,128)S(1)}, u32[]{:S(2)}, u32[]{:S(2)}) collective-permute-start(f32[2,128,128]{1,2,0:T(8,128)S(1)} %slice.250), channel_id=1, source_target_pairs={{9,0},{10,1},{11,2},{12,3},{13,4},{14,5},{15,6},{16,7},{17,8},{18,... | collective-permute-start | bytes 393224 | tf_op jit(solution)/shard_map/ppermute | solution.py:18
  70.3 133.7 %copy-start = (f32[2,128,128]{2,1,0:T(8,128)S(1)}, f32[2,128,128]{2,1,0:T(8,128)}, u32[]{:S(2)}) copy-start(f32[2,128,128]{2,1,0:T(8,128)} %probe.3) | copy-start | bytes 393220
  71.1 134.5 %collective-permute-start.9 = (f32[2,128,256]{1,2,0:T(8,128)S(1)}, f32[2,128,256]{1,2,0:T(8,128)S(1)}, u32[]{:S(2)}, u32[]{:S(2)}) collective-permute-start(f32[2,128,256]{1,2,0:T(8,128)S(1)} %slice.253), channel_id=1, source_target_pairs={{0,8},{8,16},{16,24},{1,9},{9,17},{17,25},{2,10},{10,18},{18,26},{... | collective-permute-start | bytes 786440 | tf_op jit(solution)/shard_map/ppermute | solution.py:18
  75.0 130.6 %collective-permute-start.10 = (f32[2,256,128]{1,2,0:T(8,128)S(1)}, f32[2,256,128]{1,2,0:T(8,128)}, u32[]{:S(2)}, u32[]{:S(2)}) collective-permute-start(f32[2,256,128]{1,2,0:T(8,128)S(1)} %slice.255), channel_id=1, source_target_pairs={{0,1},{1,2},{2,3},{3,4},{4,5},{5,6},{6,7},{8,9},{9,10},{10,11},{11... | collective-permute-start | bytes 786440 | tf_op jit(solution)/shard_map/ppermute | solution.py:18
  81.6 125.1 %collective-permute-start.11 = (f32[2,128,128]{1,2,0:T(8,128)}, f32[2,128,128]{1,2,0:T(8,128)S(1)}, u32[]{:S(2)}, u32[]{:S(2)}) collective-permute-start(f32[2,128,128]{1,2,0:T(8,128)} %slice.257), channel_id=1, source_target_pairs={{0,9},{1,10},{2,11},{3,12},{4,13},{5,14},{6,15},{7,16},{8,17},{9,1... | collective-permute-start | bytes 393224 | tf_op jit(solution)/shard_map/ppermute | solution.py:18
Sparse Core Ops, SparseCore 0:
  68.8 132.9 all-reduce.1

commit v2 on v1

--- a/solution.py
+++ b/solution.py
@@ -10,12 +10,6 @@
 from jax.sharding import PartitionSpec as P
 
 GROUP = 4
-
-
-def from_behind(value, axis, steps):
-    count = lax.axis_size(axis)
-    first, last = (max(0, -steps), min(count, count - steps))
-    return lax.ppermute(value, axis, [(source, source + steps) for source in range(first, last)])
 
 
 def dft_tables(window):
@@ -139,55 +133,338 @@
     )(corners, live, ext, probe, amp, ahead, back)
 
 
-def strips_of(value, window):
-    planes, rows, columns = value.shape
-    return jnp.transpose(value.reshape(planes, rows, columns // window, window), (0, 2, 1, 3))
-
-
-def extend(current, window):
-    right_rim = from_behind(current[:, :, :window], "col", -1)
-    lower_rim = from_behind(current[:, :window, :], "row", -1)
-    corner_rim = from_behind(
-        current[:, :window, :window], ("row", "col"), -(lax.axis_size("col") + 1)
-    )
-    widened = jnp.concatenate([current, right_rim], 2)
-    lower_wide = jnp.concatenate([lower_rim, corner_rim], 2)
-    return strips_of(jnp.concatenate([widened, lower_wide], 1), window)
-
-
-def fold(deposit, window):
-    deposit = jnp.transpose(deposit, (0, 2, 1, 3)).reshape(deposit.shape[0], deposit.shape[2], -1)
-    tile_size = deposit.shape[1] - window
-    spilled = from_behind(deposit[:, tile_size:, :tile_size], "row", 1)
-    right_part = from_behind(deposit[:, :tile_size, tile_size:], "col", 1)
-    corner_part = from_behind(
-        deposit[:, tile_size:, tile_size:], ("row", "col"), lax.axis_size("col") + 1
-    )
-    result = deposit[:, :tile_size, :tile_size]
-    result = result.at[:, :window, :].add(spilled)
-    result = result.at[:, :, :window].add(right_part)
-    return result.at[:, :window, :window].add(corner_part)
-
-
-def on_device(object_field, probe, amplitude, corners, live_count):
+MESH = pl.DeviceIdType.MESH
+
+
+class Place:
+    def __init__(self, rows, cols):
+        self.row, self.col = lax.axis_index("row"), lax.axis_index("col")
+        self.rows, self.cols = rows, cols
+
+    def at(self, down, right):
+        return (
+            lax.rem(self.row + down + self.rows, self.rows),
+            lax.rem(self.col + right + self.cols, self.cols),
+        )
+
+    def inside(self, down, right):
+        checks = []
+        if down:
+            checks.append(self.row < self.rows - 1 if down > 0 else self.row > 0)
+        if right:
+            checks.append(self.col < self.cols - 1 if right > 0 else self.col > 0)
+        return checks[0] if len(checks) == 1 else jnp.logical_and(*checks)
+
+
+def greet(place, steps):
+    barrier = pltpu.get_barrier_semaphore()
+    for step in steps:
+
+        @pl.when(place.inside(*step))
+        def _():
+            pl.semaphore_signal(barrier, inc=1, device_id=place.at(*step), device_id_type=MESH)
+
+    return barrier
+
+
+def meet(place, barrier, steps, others=0):
+    for step in steps:
+        others = others + jnp.where(place.inside(*step), 1, 0)
+    pl.semaphore_wait(barrier, others)
+
+
+NEAR = ((0, -1), (-1, 0), (-1, -1), (0, 1), (1, 0), (1, 1))
+
+
+class Shift:
+    def __init__(self, place, step, source, target, sems, index):
+        self.copy = pltpu.make_async_remote_copy(
+            src_ref=source,
+            dst_ref=target,
+            send_sem=sems.at[0, index],
+            recv_sem=sems.at[1, index],
+            device_id=place.at(*step),
+            device_id_type=MESH,
+        )
+        self.sends = place.inside(*step)
+        self.receives = place.inside(-step[0], -step[1])
+
+    def start(self):
+        pl.when(self.sends)(self.copy.start)
+
+    def wait_send(self):
+        pl.when(self.sends)(self.copy.wait_send)
+
+
+def rim_shifts(place, field, ext, sems, win):
+    tile = ext.shape[2] - win
+    return [
+        Shift(place, (0, -1), field(0, tile), ext.at[:, 2, pl.ds(0, tile)], sems, 0),
+        Shift(place, (-1, -1), field(0, win), ext.at[:, 2, pl.ds(tile, win)], sems, 1),
+        Shift(place, (-1, 0), field(0, win), ext.at[:, 0, pl.ds(tile, win)], sems, 2),
+        Shift(place, (-1, 0), field(1, win), ext.at[:, 1, pl.ds(tile, win)], sems, 3),
+    ]
+
+
+def spill_shifts(place, deposit, right_in, low_in, corner_in, sems, win):
+    tile = deposit.shape[2] - win
+    return [
+        Shift(place, (0, 1), deposit.at[:, 2, pl.ds(0, tile)], right_in, sems, 0),
+        Shift(place, (1, 1), deposit.at[:, 2, pl.ds(tile, win)], corner_in, sems, 1),
+        Shift(place, (1, 0), deposit.at[:, pl.ds(0, 2), pl.ds(tile, win)], low_in, sems, 2),
+    ]
+
+
+def finish(shifts):
+    for shift in shifts:
+        pl.when(shift.receives)(shift.copy.wait_recv)
+    for shift in shifts:
+        shift.wait_send()
+
+
+def extend_kernel(rows, cols, obj, ext, sems):
+    win = ext.shape[3]
+    tile = ext.shape[2] - win
+    place = Place(rows, cols)
+    barrier = greet(place, NEAR)
+    for strip in range(2):
+        ext[:, strip, :tile] = obj[:, :, strip * win : (strip + 1) * win]
+    meet(place, barrier, NEAR)
+
+    def field(strip, height):
+        return obj.at[:, pl.ds(0, height), pl.ds(strip * win, win)]
+
+    shifts = rim_shifts(place, field, ext, sems, win)
+    for shift in shifts:
+        shift.start()
+    finish(shifts)
+
+
+def update_kernel(
+    rows, cols, spread, obj, ext, inverse, right_in, low_in, corner_in, total, sems, rim_sems
+):
+    win = ext.shape[3]
+    tile = ext.shape[2] - win
+    place = Place(rows, cols)
+    barrier = greet(place, NEAR)
+    meet(place, barrier, NEAR)
+    shifts = spill_shifts(place, spread, right_in, low_in, corner_in, sems, win)
+    for shift in shifts:
+        shift.start()
+    for strip in range(2):
+        total[:, strip] = spread[:, strip, :tile]
+    side, corner, low = shifts
+
+    @pl.when(low.receives)
+    def _():
+        low.copy.wait_recv()
+        for strip in range(2):
+            total[:, strip, :win] += low_in[:, strip]
+
+    @pl.when(side.receives)
+    def _():
+        side.copy.wait_recv()
+        total[:, 0] += right_in[...]
+
+    @pl.when(corner.receives)
+    def _():
+        corner.copy.wait_recv()
+        total[:, 0, :win] += corner_in[...]
+
+    rims = rim_shifts(
+        place, lambda strip, height: ext.at[:, strip, pl.ds(0, height)], ext, rim_sems, win
+    )
+    for strip in range(2):
+        share = 1.0 / (total[2, strip] + 4.0)
+        inverse[strip] = share
+        for plane in range(2):
+            ext[plane, strip, :tile] = (
+                obj[plane, :, strip * win : (strip + 1) * win] + total[plane, strip] * share
+            )
+        for rim in rims[:3] if strip == 0 else rims[3:]:
+            rim.start()
+    for shift in shifts:
+        shift.wait_send()
+    finish(rims)
+
+
+def last_kernel(
+    rows,
+    cols,
+    spread,
+    ext,
+    inverse,
+    gradient,
+    probe,
+    refined,
+    new_probe,
+    right_in,
+    low_in,
+    corner_in,
+    part_in,
+    peer_in,
+    whole,
+    own,
+    sems,
+    part_sems,
+    peer_sems,
+    whole_sems,
+):
+    win = ext.shape[3]
+    tile = ext.shape[2] - win
+    place = Place(rows, cols)
+    diagonal = ((-1, -1), (1, 1))
+    barrier = greet(place, diagonal)
+    col_peers = [place.at(0, step) for step in range(1, cols)]
+    row_peers = [place.at(step, 0) for step in range(1, rows)]
+    for peer in col_peers + row_peers:
+        pl.semaphore_signal(barrier, inc=1, device_id=peer, device_id_type=MESH)
+    meet(place, barrier, diagonal, cols + rows - 2)
+    height = whole.shape[0] // cols
+
+    def piece(index):
+        return pl.ds(pl.multiple_of(index * height, height), height)
+
+    def send(source, target, pair, index, peer):
+        copy = pltpu.make_async_remote_copy(
+            src_ref=source,
+            dst_ref=target,
+            send_sem=pair.at[0, index],
+            recv_sem=pair.at[1, index],
+            device_id=peer,
+            device_id_type=MESH,
+        )
+        copy.start()
+        return copy
+
+    parts = [
+        send(gradient.at[piece(peer[1])], part_in.at[index], part_sems, index, peer)
+        for index, peer in enumerate(col_peers)
+    ]
+    shifts = spill_shifts(place, spread, right_in, low_in, corner_in, sems, win)
+    for shift in shifts:
+        shift.start()
+    summed = gradient[piece(place.col)]
+    for index, copy in enumerate(parts):
+        copy.wait_recv()
+        summed = summed + part_in[index]
+    own[...] = summed
+    peer_in[place.row] = summed
+    peers = [
+        send(own, peer_in.at[place.row], peer_sems, index, peer)
+        for index, peer in enumerate(row_peers)
+    ]
+    for copy in peers:
+        copy.wait_recv()
+    summed = peer_in[0]
+    for index in range(1, rows):
+        summed = summed + peer_in[index]
+    whole[piece(place.col)] = summed
+    gathers = [
+        send(whole.at[piece(place.col)], whole.at[piece(place.col)], whole_sems, index, peer)
+        for index, peer in enumerate(col_peers)
+    ]
+    for strip in range(2):
+        for plane in range(2):
+            refined[plane, :, strip * win : (strip + 1) * win] = spread[plane, strip, :tile]
+    side, corner, low = shifts
+
+    @pl.when(low.receives)
+    def _():
+        low.copy.wait_recv()
+        for strip in range(2):
+            refined[:, :win, strip * win : (strip + 1) * win] += low_in[:, strip]
+
+    @pl.when(side.receives)
+    def _():
+        side.copy.wait_recv()
+        refined[:, :, :win] += right_in[...]
+
+    @pl.when(corner.receives)
+    def _():
+        corner.copy.wait_recv()
+        refined[:, :win, :win] += corner_in[...]
+
+    for strip in range(2):
+        columns = slice(strip * win, (strip + 1) * win)
+        for plane in range(2):
+            refined[plane, :, columns] = (
+                ext[plane, strip, :tile] + refined[plane, :, columns] * inverse[strip]
+            )
+    for copy in gathers:
+        copy.wait_recv()
+    total = whole[...]
+    power = jnp.sum(total * total, axis=(0, 1), keepdims=True) / (total.shape[0] // 2 * win)
+    new_probe[...] = probe[...] + total * lax.rsqrt(power + 1e-06)
+    for copy in parts + peers + gathers:
+        copy.wait_send()
+    for shift in shifts:
+        shift.wait_send()
+
+
+def remote_call(kernel, ident, out_shape, scratch, operands):
+    vmem = pl.BlockSpec(memory_space=pltpu.VMEM)
+    return pl.pallas_call(
+        kernel,
+        out_shape=out_shape,
+        in_specs=[vmem] * len(operands),
+        out_specs=[vmem] * len(out_shape),
+        scratch_shapes=scratch,
+        compiler_params=pltpu.CompilerParams(collective_id=ident, has_side_effects=True),
+    )(*operands)
+
+
+def on_device(rows, cols, object_field, probe, amplitude, corners, live_count):
     slots = amplitude.shape[2]
-    window = probe.shape[1]
-    amp = amplitude.reshape(slots, window, window)
+    win = probe.shape[1]
+    tile = object_field.shape[1]
+    amp = amplitude.reshape(slots, win, win)
     corners = corners.reshape(2, slots)
     live = live_count.reshape(1)
-    ahead, back = dft_tables(window)
-    (deposit,) = sweep(True, corners, live, extend(object_field, window), probe, amp, ahead, back)
-    first_pass = fold(deposit, window)
-    denominator = first_pass[2] + 4.0
-    updated = object_field + first_pass[:2] / denominator
-    deposit, gradient = sweep(
-        False, corners, live, extend(updated, window), probe, amp, ahead, back
-    )
-    refined_object = updated + fold(deposit, window) / denominator
-    summed = lax.psum(gradient, ("row", "col"))
-    spread = jnp.sqrt(jnp.mean(summed[0] * summed[0] + summed[1] * summed[1]) + 1e-06)
-    new_probe = probe + summed / spread
-    return (refined_object, new_probe)
+    ahead, back = dft_tables(win)
+    f32 = jnp.float32
+    sem = pltpu.SemaphoreType.DMA
+    ext_shape = jax.ShapeDtypeStruct((2, tile // win + 1, tile + win, win), f32)
+
+    def inboxes(planes):
+        return [
+            pltpu.VMEM((planes, tile, win), f32),
+            pltpu.VMEM((planes, 2, win, win), f32),
+            pltpu.VMEM((planes, win, win), f32),
+        ]
+
+    (ext,) = remote_call(
+        functools.partial(extend_kernel, rows, cols), 0, [ext_shape], [sem((2, 4))], [object_field]
+    )
+    (spread,) = sweep(True, corners, live, ext, probe, amp, ahead, back)
+    ext, inverse = remote_call(
+        functools.partial(update_kernel, rows, cols),
+        1,
+        [ext_shape, jax.ShapeDtypeStruct((2, tile, win), f32)],
+        inboxes(3) + [pltpu.VMEM((3, 2, tile, win), f32), sem((2, 3)), sem((2, 4))],
+        [spread, object_field],
+    )
+    spread, gradient = sweep(False, corners, live, ext, probe, amp, ahead, back)
+    flat = (2 * win, win)
+    height = 2 * win // cols
+    refined, new_probe = remote_call(
+        functools.partial(last_kernel, rows, cols),
+        2,
+        [jax.ShapeDtypeStruct(object_field.shape, f32), jax.ShapeDtypeStruct(flat, f32)],
+        inboxes(2)
+        + [
+            pltpu.VMEM((cols - 1, height, win), f32),
+            pltpu.VMEM((rows, height, win), f32),
+            pltpu.VMEM(flat, f32),
+            pltpu.VMEM((height, win), f32),
+            sem((2, 3)),
+            sem((2, cols - 1)),
+            sem((2, rows - 1)),
+            sem((2, cols - 1)),
+        ],
+        [spread, ext, inverse, gradient.reshape(flat), probe.reshape(flat)],
+    )
+    return (refined, new_probe.reshape(probe.shape))
 
 
 def solution(mesh):
@@ -200,5 +477,5 @@
     )
     out_specs = (P(None, "row", "col"), P())
     return jax.shard_map(
-        on_device, mesh=mesh, in_specs=in_specs, out_specs=out_specs, check_vma=False
-    )
+        functools.partial(on_device, mesh.shape["row"], mesh.shape["col"]), mesh=mesh, in_specs=in_specs, out_specs=out_specs, check_vma=False
+    )

time: 214 us -> 81.8 us (0.38)
  waiting for transfers between devices: 140 us -> 0 us
  Pallas kernels: 10.2 us -> 76.5 us
  starting transfers between devices: 34 us -> 0 us
  between operations: 15.7 us -> 1.3 us
  local copies, waits for them, and re-layouts: 9.86 us -> 3.44 us
  other arithmetic: 4.74 us -> 0 us
    psum x1 -> x0, waiting for transfers between devices: 117 us -> none  [on_device(): summed = lax.psum(gradient, ('row', 'col'))]
    pallas_call x0 -> x3, Pallas kernels: none -> 61.7 us  [remote_call(): pl.pallas_call(kernel, out_shape=out_shape, in_specs=[vmem] * len(operand...]
    ppermute x12 -> x0, starting transfers between devices: 34 us -> none  [from_behind(): lax.ppermute(value, axis, [(source, source + steps) for source in range(f...]
    ppermute x12 -> x0, waiting for transfers between devices: 23.2 us -> none  [from_behind(): lax.ppermute(value, axis, [(source, source + steps) for source in range(f...]
    pallas_call x2, Pallas kernels: 10.2 us -> 14.8 us  [sweep(): pl.pallas_call(functools.partial(sweep_kernel, with_light), out_shape=out...]
    transpose x2 -> x0, local copies, waits for them, and re-layouts: 3.86 us -> none  [fold(): jnp.transpose(deposit, (0, 2, 1, 3))]
    reshape x2 -> x0, local copies, waits for them, and re-layouts: 2.79 us -> none  [strips_of(): value.reshape(planes, rows, columns // window, window)]
  transfers between devices with their start and end apart: 13 -> 0, of which waited for: 5 -> 0; matrix products, arithmetic and copies ran while one was open for 3% -> 0% of each run, Pallas kernels for 0% -> 0%
where the time goes in v2:
time: 81.8 us; the launch traced here: 81.2 us
  Pallas kernels  76.5 us (94%)
  local copies, waits for them, and re-layouts  3.44 us (4%)
  between operations  1.3 us (2%)
    pallas_call x3, Pallas kernels, remote_call(): pl.pallas_call(kernel, out_shape=out_shape, in_specs=[vmem] * len(operand...  61.7 us
    pallas_call x2, Pallas kernels, sweep(): pl.pallas_call(functools.partial(sweep_kernel, with_light), out_shape=out...  14.8 us
    unnamed x2, local copies, waits for them, and re-layouts  3.44 us

profile of v2, /device:TPU:0, one launch (start us, length us, event | category | flops | bytes accessed | tf_op | source)
XLA Modules:
  0.0 81.2 jit_solution(844006487608687538)
XLA Ops:
  1.3 16.6 %shard_map.86.ext = f32[2,3,384,128]{3,2,1,0:T(8,128)} custom-call(f32[2,256,256]{2,1,0:T(8,128)} %obj.3), custom_call_target="tpu_custom_call" | custom-call | tf_op jit(solution)/shard_map/pallas_call | solution.py:407
  17.9 7.4 %first_sweep.1.spread = f32[3,3,384,128]{3,2,1,0:T(8,128)} custom-call(s32[2,16]{1,0:T(2,128)} %bitcast.13, s32[1]{0:T(128)} %bitcast.6.live, f32[2,3,384,128]{3,2,1,0:T(8,128)} %shard_map.86.ext, f32[2,128,128]{2,1,0:T(8,128)} %probe.3, bf16[16,128,128]{2,1,0:T(8,128)(2,1)} %bitcast.8, bf16[256,256]{1,0:T(8,128)(2,1)} %constant.4.clone.ahead, ...), custom_call_target="tpu_custom_call" | custom-call | tf_op jit(solution)/shard_map/first_sweep/pallas_call | solution.py:126
  25.3 24.1 %shard_map.87 = (f32[2,3,384,128]{3,2,1,0:T(8,128)}, f32[2,256,128]{2,1,0:T(8,128)}) custom-call(f32[3,3,384,128]{3,2,1,0:T(8,128)} %first_sweep.1.spread, f32[2,256,256]{2,1,0:T(8,128)} %obj.3), custom_call_target="tpu_custom_call" | custom-call | tf_op jit(solution)/shard_map/pallas_call | solution.py:407
  49.4 7.3 %second_sweep.1 = (f32[2,3,384,128]{3,2,1,0:T(8,128)}, f32[2,128,128]{2,1,0:T(8,128)}) custom-call(s32[2,16]{1,0:T(2,128)} %bitcast.14, s32[1]{0:T(128)} %bitcast.7.live, f32[2,3,384,128]{3,2,1,0:T(8,128)} %get-tuple-element.8.ext, f32[2,128,128]{2,1,0:T(8,128)} %probe.3, bf16[16,128,128]{2,1,0:T(8,128)(2,1)} %bitcast.9, ...), custom_call_target="tpu_custom_call" | custom-call | tf_op jit(solution)/shard_map/second_sweep/pallas_call | solution.py:126
  56.8 21.0 %shard_map.88 = (f32[2,256,256]{2,1,0:T(8,128)}, f32[256,128]{1,0:T(8,128)}) custom-call(f32[2,3,384,128]{3,2,1,0:T(8,128)} %get-tuple-element.9.spread, f32[2,3,384,128]{3,2,1,0:T(8,128)} %get-tuple-element.8.ext, f32[2,256,128]{2,1,0:T(8,128)} %get-tuple-element.10.inverse, f32[256,128]{1,0:T(8,128)} %bitcast.11, f32[256,128]{1,0:T(8,128)} %bitcast.10), custom_call_target="tpu_custom_call" | custom-call | tf_op jit(solution)/shard_map/pallas_call | solution.py:407
  77.8 1.9 %copy.12 = f32[2,256,256]{2,1,0:T(8,128)} copy(f32[2,256,256]{2,1,0:T(8,128)} %get-tuple-element.16) | data formatting | bytes 1048576
  79.6 1.6 %copy.13 = f32[2,128,128]{2,1,0:T(8,128)} copy(f32[2,128,128]{2,1,0:T(8,128)} %bitcast.12) | data formatting | bytes 262144

commit v3 on v2

--- a/solution.py
+++ b/solution.py
@@ -28,10 +28,11 @@
 
 
 def sweep_kernel(with_light, corners, live, ext, probe, amp, ahead, back, deposit, *rest):
+    side_out, low_out, corner_out = rest[:3]
     if with_light:
-        waves_buf = rest[0]
+        waves_buf = rest[3]
     else:
-        gradient, waves_buf, patch_buf = rest
+        gradient, narrow, waves_buf, patch_buf = rest[3:]
         gradient[...] = jnp.zeros_like(gradient)
     slots, win = amp.shape[0], amp.shape[1]
     deposit[...] = jnp.zeros_like(deposit)
@@ -111,6 +112,17 @@
                 gradient[0] += ore * re + oim * im
                 gradient[1] += ore * im - oim * re
 
+    tile = deposit.shape[2] - win
+    side_out[...] = deposit[:, 2, :tile].astype(jnp.bfloat16)
+    low_out[...] = deposit[:, :2, tile:].astype(jnp.bfloat16)
+    corner_out[...] = deposit[:, 2, tile:].astype(jnp.bfloat16)
+    if not with_light:
+        narrow[...] = gradient[...].astype(jnp.bfloat16)
+
+
+def spill_shapes(planes, tile, win):
+    return [(planes, tile, win), (planes, 2, win, win), (planes, win, win)]
+
 
 def sweep(with_light, corners, live, ext, probe, amp, ahead, back):
     slots, win = amp.shape[0], amp.shape[1]
@@ -119,9 +131,12 @@
     smem = pl.BlockSpec(memory_space=pltpu.SMEM)
     planes = 3 if with_light else 2
     out_shape = [jax.ShapeDtypeStruct((planes, strips, side, win), jnp.float32)]
+    for shape in spill_shapes(planes, side - win, win):
+        out_shape.append(jax.ShapeDtypeStruct(shape, jnp.bfloat16))
     scratch = [pltpu.VMEM((GROUP * win, 2 * win), jnp.bfloat16)]
     if not with_light:
         out_shape.append(jax.ShapeDtypeStruct((2, win, win), jnp.float32))
+        out_shape.append(jax.ShapeDtypeStruct((2, win, win), jnp.bfloat16))
         scratch.append(pltpu.VMEM((GROUP, 2, win, win), jnp.float32))
     return pl.pallas_call(
         functools.partial(sweep_kernel, with_light),
@@ -196,120 +211,132 @@
         pl.when(self.sends)(self.copy.wait_send)
 
 
-def rim_shifts(place, field, ext, sems, win):
-    tile = ext.shape[2] - win
+def box_shifts(place, down, side, low, corner, sems):
     return [
-        Shift(place, (0, -1), field(0, tile), ext.at[:, 2, pl.ds(0, tile)], sems, 0),
-        Shift(place, (-1, -1), field(0, win), ext.at[:, 2, pl.ds(tile, win)], sems, 1),
-        Shift(place, (-1, 0), field(0, win), ext.at[:, 0, pl.ds(tile, win)], sems, 2),
-        Shift(place, (-1, 0), field(1, win), ext.at[:, 1, pl.ds(tile, win)], sems, 3),
+        Shift(place, (0, down), *side, sems, 0),
+        Shift(place, (down, down), *corner, sems, 1),
+        Shift(place, (down, 0), *low, sems, 2),
     ]
 
 
-def spill_shifts(place, deposit, right_in, low_in, corner_in, sems, win):
-    tile = deposit.shape[2] - win
-    return [
-        Shift(place, (0, 1), deposit.at[:, 2, pl.ds(0, tile)], right_in, sems, 0),
-        Shift(place, (1, 1), deposit.at[:, 2, pl.ds(tile, win)], corner_in, sems, 1),
-        Shift(place, (1, 0), deposit.at[:, pl.ds(0, 2), pl.ds(tile, win)], low_in, sems, 2),
-    ]
-
-
-def finish(shifts):
-    for shift in shifts:
-        pl.when(shift.receives)(shift.copy.wait_recv)
+def finish_sends(shifts):
     for shift in shifts:
         shift.wait_send()
 
 
-def extend_kernel(rows, cols, obj, ext, sems):
+def arrive(shifts, side, low, corner):
+    for shift, action in zip((shifts[2], shifts[0], shifts[1]), (low, side, corner)):
+
+        @pl.when(shift.receives)
+        def _():
+            shift.copy.wait_recv()
+            action()
+
+
+def fill_rims(shifts, ext, side_in, low_in, corner_in):
+    win = ext.shape[3]
+    tile = ext.shape[2] - win
+
+    def low():
+        ext[:, :2, tile:] = low_in[...].astype(jnp.float32)
+
+    def side():
+        ext[:, 2, :tile] = side_in[...].astype(jnp.float32)
+
+    def corner():
+        ext[:, 2, tile:] = corner_in[...].astype(jnp.float32)
+
+    arrive(shifts, side, low, corner)
+
+
+def add_spills(shifts, total, side_in, low_in, corner_in):
+    win = total.shape[3]
+
+    def low():
+        total[:, :, :win] += low_in[...].astype(jnp.float32)
+
+    def side():
+        total[:, 0] += side_in[...].astype(jnp.float32)
+
+    def corner():
+        total[:, 0, :win] += corner_in[...].astype(jnp.float32)
+
+    arrive(shifts, side, low, corner)
+
+
+def rim_boxes(place, outs, ins, win, sems):
+    side_out, low_out = outs
+    side_in, low_in, corner_in = ins
+    return box_shifts(
+        place,
+        -1,
+        (side_out, side_in),
+        (low_out, low_in),
+        (side_out.at[:, pl.ds(0, win)], corner_in),
+        sems,
+    )
+
+
+def extend_kernel(rows, cols, obj, ext, side_out, low_out, side_in, low_in, corner_in, sems):
     win = ext.shape[3]
     tile = ext.shape[2] - win
     place = Place(rows, cols)
     barrier = greet(place, NEAR)
+    side_out[...] = obj[:, :, :win].astype(jnp.bfloat16)
+    for strip in range(2):
+        low_out[:, strip] = obj[:, :win, strip * win : (strip + 1) * win].astype(jnp.bfloat16)
+    meet(place, barrier, NEAR)
+    shifts = rim_boxes(place, (side_out, low_out), (side_in, low_in, corner_in), win, sems)
+    for shift in shifts:
+        shift.start()
     for strip in range(2):
         ext[:, strip, :tile] = obj[:, :, strip * win : (strip + 1) * win]
-    meet(place, barrier, NEAR)
-
-    def field(strip, height):
-        return obj.at[:, pl.ds(0, height), pl.ds(strip * win, win)]
-
-    shifts = rim_shifts(place, field, ext, sems, win)
-    for shift in shifts:
-        shift.start()
-    finish(shifts)
-
-
-def update_kernel(
-    rows, cols, spread, obj, ext, inverse, right_in, low_in, corner_in, total, sems, rim_sems
-):
+    fill_rims(shifts, ext, side_in, low_in, corner_in)
+    finish_sends(shifts)
+
+
+def update_kernel(rows, cols, *refs):
+    spread, side_spill, low_spill, corner_spill, obj, ext, inverse = refs[:7]
+    side_got, low_got, corner_got, side_out, low_out, side_in, low_in, corner_in = refs[7:15]
+    total, sems, rim_sems = refs[15:]
     win = ext.shape[3]
     tile = ext.shape[2] - win
     place = Place(rows, cols)
     barrier = greet(place, NEAR)
     meet(place, barrier, NEAR)
-    shifts = spill_shifts(place, spread, right_in, low_in, corner_in, sems, win)
-    for shift in shifts:
+    spills = box_shifts(
+        place,
+        1,
+        (side_spill, side_got),
+        (low_spill, low_got),
+        (corner_spill, corner_got),
+        sems,
+    )
+    for shift in spills:
         shift.start()
-    for strip in range(2):
-        total[:, strip] = spread[:, strip, :tile]
-    side, corner, low = shifts
-
-    @pl.when(low.receives)
-    def _():
-        low.copy.wait_recv()
-        for strip in range(2):
-            total[:, strip, :win] += low_in[:, strip]
-
-    @pl.when(side.receives)
-    def _():
-        side.copy.wait_recv()
-        total[:, 0] += right_in[...]
-
-    @pl.when(corner.receives)
-    def _():
-        corner.copy.wait_recv()
-        total[:, 0, :win] += corner_in[...]
-
-    rims = rim_shifts(
-        place, lambda strip, height: ext.at[:, strip, pl.ds(0, height)], ext, rim_sems, win
-    )
+    total[...] = spread[:, :2, :tile]
+    add_spills(spills, total, side_got, low_got, corner_got)
+    rims = rim_boxes(place, (side_out, low_out), (side_in, low_in, corner_in), win, rim_sems)
     for strip in range(2):
         share = 1.0 / (total[2, strip] + 4.0)
+        for plane in range(2):
+            fresh = obj[plane, :, strip * win : (strip + 1) * win] + total[plane, strip] * share
+            if strip == 0:
+                side_out[plane] = fresh.astype(jnp.bfloat16)
+            low_out[plane, strip] = fresh[:win].astype(jnp.bfloat16)
+            ext[plane, strip, :tile] = fresh
         inverse[strip] = share
-        for plane in range(2):
-            ext[plane, strip, :tile] = (
-                obj[plane, :, strip * win : (strip + 1) * win] + total[plane, strip] * share
-            )
-        for rim in rims[:3] if strip == 0 else rims[3:]:
+        for rim in rims[:2] if strip == 0 else rims[2:]:
             rim.start()
-    for shift in shifts:
-        shift.wait_send()
-    finish(rims)
-
-
-def last_kernel(
-    rows,
-    cols,
-    spread,
-    ext,
-    inverse,
-    gradient,
-    probe,
-    refined,
-    new_probe,
-    right_in,
-    low_in,
-    corner_in,
-    part_in,
-    peer_in,
-    whole,
-    own,
-    sems,
-    part_sems,
-    peer_sems,
-    whole_sems,
-):
+    finish_sends(spills)
+    fill_rims(rims, ext, side_in, low_in, corner_in)
+    finish_sends(rims)
+
+
+def last_kernel(rows, cols, *refs):
+    spread, side_spill, low_spill, corner_spill, ext, inverse, gradient, narrow, probe = refs[:9]
+    refined, new_probe, side_got, low_got, corner_got, total = refs[9:15]
+    part_in, peer_in, whole, own, sems, part_sems, peer_sems, whole_sems = refs[15:]
     win = ext.shape[3]
     tile = ext.shape[2] - win
     place = Place(rows, cols)
@@ -320,7 +347,7 @@
     for peer in col_peers + row_peers:
         pl.semaphore_signal(barrier, inc=1, device_id=peer, device_id_type=MESH)
     meet(place, barrier, diagonal, cols + rows - 2)
-    height = whole.shape[0] // cols
+    height = whole.shape[0] // rows
 
     def piece(index):
         return pl.ds(pl.multiple_of(index * height, height), height)
@@ -338,68 +365,54 @@
         return copy
 
     parts = [
-        send(gradient.at[piece(peer[1])], part_in.at[index], part_sems, index, peer)
+        send(narrow.at[piece(peer[0])], part_in.at[index], part_sems, index, peer)
+        for index, peer in enumerate(row_peers)
+    ]
+    spills = box_shifts(
+        place,
+        1,
+        (side_spill, side_got),
+        (low_spill, low_got),
+        (corner_spill, corner_got),
+        sems,
+    )
+    for shift in spills:
+        shift.start()
+    summed = gradient[piece(place.row)]
+    for index, copy in enumerate(parts):
+        copy.wait_recv()
+        summed = summed + part_in[index].astype(jnp.float32)
+    own[...] = summed.astype(jnp.bfloat16)
+    peer_in[place.col] = summed.astype(jnp.bfloat16)
+    peers = [
+        send(own, peer_in.at[place.col], peer_sems, index, peer)
         for index, peer in enumerate(col_peers)
     ]
-    shifts = spill_shifts(place, spread, right_in, low_in, corner_in, sems, win)
-    for shift in shifts:
-        shift.start()
-    summed = gradient[piece(place.col)]
-    for index, copy in enumerate(parts):
+    total[...] = spread[:, :2, :tile]
+    for copy in peers:
         copy.wait_recv()
-        summed = summed + part_in[index]
-    own[...] = summed
-    peer_in[place.row] = summed
-    peers = [
-        send(own, peer_in.at[place.row], peer_sems, index, peer)
+    summed = peer_in[0].astype(jnp.float32)
+    for index in range(1, cols):
+        summed = summed + peer_in[index].astype(jnp.float32)
+    whole[piece(place.row)] = summed
+    gathers = [
+        send(whole.at[piece(place.row)], whole.at[piece(place.row)], whole_sems, index, peer)
         for index, peer in enumerate(row_peers)
     ]
-    for copy in peers:
-        copy.wait_recv()
-    summed = peer_in[0]
-    for index in range(1, rows):
-        summed = summed + peer_in[index]
-    whole[piece(place.col)] = summed
-    gathers = [
-        send(whole.at[piece(place.col)], whole.at[piece(place.col)], whole_sems, index, peer)
-        for index, peer in enumerate(col_peers)
-    ]
+    add_spills(spills, total, side_got, low_got, corner_got)
     for strip in range(2):
         for plane in range(2):
-            refined[plane, :, strip * win : (strip + 1) * win] = spread[plane, strip, :tile]
-    side, corner, low = shifts
-
-    @pl.when(low.receives)
-    def _():
-        low.copy.wait_recv()
-        for strip in range(2):
-            refined[:, :win, strip * win : (strip + 1) * win] += low_in[:, strip]
-
-    @pl.when(side.receives)
-    def _():
-        side.copy.wait_recv()
-        refined[:, :, :win] += right_in[...]
-
-    @pl.when(corner.receives)
-    def _():
-        corner.copy.wait_recv()
-        refined[:, :win, :win] += corner_in[...]
-
-    for strip in range(2):
-        columns = slice(strip * win, (strip + 1) * win)
-        for plane in range(2):
-            refined[plane, :, columns] = (
-                ext[plane, strip, :tile] + refined[plane, :, columns] * inverse[strip]
+            refined[plane, :, strip * win : (strip + 1) * win] = (
+                ext[plane, strip, :tile] + total[plane, strip] * inverse[strip]
             )
     for copy in gathers:
         copy.wait_recv()
-    total = whole[...]
-    power = jnp.sum(total * total, axis=(0, 1), keepdims=True) / (total.shape[0] // 2 * win)
-    new_probe[...] = probe[...] + total * lax.rsqrt(power + 1e-06)
+    value = whole[...]
+    power = jnp.sum(value * value, axis=(0, 1), keepdims=True) / (value.shape[0] // 2 * win)
+    new_probe[...] = probe[...] + value * lax.rsqrt(power + 1e-06)
     for copy in parts + peers + gathers:
         copy.wait_send()
-    for shift in shifts:
-        shift.wait_send()
+    finish_sends(spills)
 
 
 def remote_call(kernel, ident, out_shape, scratch, operands):
@@ -422,47 +435,59 @@
     corners = corners.reshape(2, slots)
     live = live_count.reshape(1)
     ahead, back = dft_tables(win)
-    f32 = jnp.float32
+    f32, b16 = jnp.float32, jnp.bfloat16
     sem = pltpu.SemaphoreType.DMA
     ext_shape = jax.ShapeDtypeStruct((2, tile // win + 1, tile + win, win), f32)
 
-    def inboxes(planes):
-        return [
-            pltpu.VMEM((planes, tile, win), f32),
-            pltpu.VMEM((planes, 2, win, win), f32),
-            pltpu.VMEM((planes, win, win), f32),
-        ]
+    def boxes(planes, count=3):
+        return [pltpu.VMEM(shape, b16) for shape in spill_shapes(planes, tile, win)[:count]]
 
     (ext,) = remote_call(
-        functools.partial(extend_kernel, rows, cols), 0, [ext_shape], [sem((2, 4))], [object_field]
-    )
-    (spread,) = sweep(True, corners, live, ext, probe, amp, ahead, back)
+        functools.partial(extend_kernel, rows, cols),
+        0,
+        [ext_shape],
+        boxes(2, 2) + boxes(2) + [sem((2, 3))],
+        [object_field],
+    )
+    spread, *spills = sweep(True, corners, live, ext, probe, amp, ahead, back)
     ext, inverse = remote_call(
         functools.partial(update_kernel, rows, cols),
         1,
         [ext_shape, jax.ShapeDtypeStruct((2, tile, win), f32)],
-        inboxes(3) + [pltpu.VMEM((3, 2, tile, win), f32), sem((2, 3)), sem((2, 4))],
-        [spread, object_field],
-    )
-    spread, gradient = sweep(False, corners, live, ext, probe, amp, ahead, back)
+        boxes(3)
+        + boxes(2, 2)
+        + boxes(2)
+        + [pltpu.VMEM((3, 2, tile, win), f32), sem((2, 3)), sem((2, 3))],
+        [spread, *spills, object_field],
+    )
+    spread, *spills, gradient, narrow = sweep(False, corners, live, ext, probe, amp, ahead, back)
     flat = (2 * win, win)
-    height = 2 * win // cols
+    height = 2 * win // rows
     refined, new_probe = remote_call(
         functools.partial(last_kernel, rows, cols),
         2,
         [jax.ShapeDtypeStruct(object_field.shape, f32), jax.ShapeDtypeStruct(flat, f32)],
-        inboxes(2)
+        boxes(2)
         + [
-            pltpu.VMEM((cols - 1, height, win), f32),
-            pltpu.VMEM((rows, height, win), f32),
+            pltpu.VMEM((2, 2, tile, win), f32),
+            pltpu.VMEM((rows - 1, height, win), b16),
+            pltpu.VMEM((cols, height, win), b16),
             pltpu.VMEM(flat, f32),
-            pltpu.VMEM((height, win), f32),
+            pltpu.VMEM((height, win), b16),
             sem((2, 3)),
+            sem((2, rows - 1)),
             sem((2, cols - 1)),
             sem((2, rows - 1)),
-            sem((2, cols - 1)),
         ],
-        [spread, ext, inverse, gradient.reshape(flat), probe.reshape(flat)],
+        [
+            spread,
+            *spills,
+            ext,
+            inverse,
+            gradient.reshape(flat),
+            narrow.reshape(flat),
+            probe.reshape(flat),
+        ],
     )
     return (refined, new_probe.reshape(probe.shape))
 

time: 81.8 us -> 64.7 us (0.79); the launches traced: 81.2 us -> 65.1 us
  Pallas kernels: 76.5 us -> 60.3 us
    pallas_call x3, Pallas kernels: 61.7 us -> 49.9 us  [remote_call(): pl.pallas_call(kernel, out_shape=out_shape, in_specs=[vmem] * len(operand...]
    pallas_call x2, Pallas kernels: 14.8 us -> 10.4 us  [sweep(): pl.pallas_call(functools.partial(sweep_kernel, with_light), out_shape=out...]
where the time goes in v3:
time: 64.7 us; the launch traced here: 65.1 us
  Pallas kernels  60.3 us (93%)
  local copies, waits for them, and re-layouts  3.44 us (5%)
  between operations  1.3 us (2%)
    pallas_call x3, Pallas kernels, remote_call(): pl.pallas_call(kernel, out_shape=out_shape, in_specs=[vmem] * len(operand...  49.9 us
    pallas_call x2, Pallas kernels, sweep(): pl.pallas_call(functools.partial(sweep_kernel, with_light), out_shape=out...  10.4 us
    unnamed x2, local copies, waits for them, and re-layouts  3.44 us

profile of v3, /device:TPU:0, one launch (start us, length us, event | category | flops | bytes accessed | tf_op | source)
XLA Modules:
  0.0 65.1 jit_solution(13698838320222233670)
XLA Ops:
  1.3 12.4 %shard_map.86.ext = f32[2,3,384,128]{3,2,1,0:T(8,128)} custom-call(f32[2,256,256]{2,1,0:T(8,128)} %refs_4_.1), custom_call_target="tpu_custom_call" | custom-call | tf_op jit(solution)/shard_map/pallas_call | solution.py:420
  13.7 5.3 %first_sweep.1 = (f32[3,3,384,128]{3,2,1,0:T(8,128)}, bf16[3,256,128]{2,1,0:T(8,128)(2,1)}, bf16[3,2,128,128]{3,2,1,0:T(8,128)(2,1)}, bf16[3,128,128]{2,1,0:T(8,128)(2,1)}) custom-call(s32[2,16]{1,0:T(2,128)} %bitcast.15, s32[1]{0:T(128)} %bitcast.7.live, f32[2,3,384,128]{3,2,1,0:T(8,128)} %shard_map.86.ext, f32[2,128,128]{2,1,0:T(8,128)} %probe.3, ...), custom_call_target="tpu_custom_call" | custom-call | tf_op jit(solution)/shard_map/first_sweep/pallas_call | solution.py:141
  19.0 17.2 %shard_map.87 = (f32[2,3,384,128]{3,2,1,0:T(8,128)}, f32[2,256,128]{2,1,0:T(8,128)}) custom-call(f32[3,3,384,128]{3,2,1,0:T(8,128)} %get-tuple-element.16.refs_0_, bf16[3,256,128]{2,1,0:T(8,128)(2,1)} %get-tuple-element.17.refs_1_, bf16[3,2,128,128]{3,2,1,0:T(8,128)(2,1)} %get-tuple-element.18.refs_2_, bf16[3,128,128]{2,1,0:T(8,128)(2,1)} %get-tuple-element.19.refs_3_, ...), custom_call_target="tpu_custom_call" | custom-call | tf_op jit(solution)/shard_map/pallas_call | solution.py:420
  36.2 5.1 %second_sweep.1 = (f32[2,3,384,128]{3,2,1,0:T(8,128)}, bf16[2,256,128]{2,1,0:T(8,128)(2,1)}, bf16[2,2,128,128]{3,2,1,0:T(8,128)(2,1)}, bf16[2,128,128]{2,1,0:T(8...) custom-call(s32[2,16]{1,0:T(2,128)} %bitcast.16, s32[1]{0:T(128)} %bitcast.8.live, ...), custom_call_target="tpu_custom_call" | custom-call | tf_op jit(solution)/shard_map/second_sweep/pallas_call | solution.py:141
  41.3 20.3 %shard_map.88 = (f32[2,256,256]{2,1,0:T(8,128)}, f32[256,128]{1,0:T(8,128)}) custom-call(f32[2,3,384,128]{3,2,1,0:T(8,128)} %get-tuple-element.21.refs_0_, bf16[2,256,128]{2,1,0:T(8,128)(2,1)} %get-tuple-element.22.refs_1_, bf16[2,2,128,128]{3,2,1,0:T(8,128)(2,1)} %get-tuple-element.23.refs_2_, bf16[2,128,128]{2,1,0:T(8,128)(2,1)} %get-tuple-element.24.refs_3_, ...), custom_call_target="tpu_custom_call" | custom-call | tf_op jit(solution)/shard_map/pallas_call | solution.py:420
  61.6 1.9 %copy.12 = f32[2,256,256]{2,1,0:T(8,128)} copy(f32[2,256,256]{2,1,0:T(8,128)} %get-tuple-element.32) | data formatting | bytes 1048576
  63.5 1.6 %copy.13 = f32[2,128,128]{2,1,0:T(8,128)} copy(f32[2,128,128]{2,1,0:T(8,128)} %bitcast.13) | data formatting | bytes 262144

commit v4 on v3

--- a/solution.py
+++ b/solution.py
@@ -10,6 +10,7 @@
 from jax.sharding import PartitionSpec as P
 
 GROUP = 4
+GRANT = 12 << 20
 
 
 def dft_tables(window):
@@ -144,6 +145,7 @@
         in_specs=[smem, smem] + [vmem] * 5,
         out_specs=[vmem] * len(out_shape),
         scratch_shapes=scratch,
+        compiler_params=pltpu.CompilerParams(vmem_limit_bytes=GRANT),
         name="first_sweep" if with_light else "second_sweep",
     )(corners, live, ext, probe, amp, ahead, back)
 
@@ -334,11 +336,10 @@
 
 
 def last_kernel(rows, cols, *refs):
-    spread, side_spill, low_spill, corner_spill, ext, inverse, gradient, narrow, probe = refs[:9]
-    refined, new_probe, side_got, low_got, corner_got, total = refs[9:15]
-    part_in, peer_in, whole, own, sems, part_sems, peer_sems, whole_sems = refs[15:]
-    win = ext.shape[3]
-    tile = ext.shape[2] - win
+    spread, side_spill, low_spill, corner_spill, gradient, narrow = refs[:6]
+    total, whole, side_got, low_got, corner_got = refs[6:11]
+    part_in, peer_in, own, sems, part_sems, peer_sems, whole_sems = refs[11:]
+    tile = total.shape[2]
     place = Place(rows, cols)
     diagonal = ((-1, -1), (1, 1))
     barrier = greet(place, diagonal)
@@ -400,19 +401,24 @@
         for index, peer in enumerate(row_peers)
     ]
     add_spills(spills, total, side_got, low_got, corner_got)
+    for copy in gathers:
+        copy.wait_recv()
+    for copy in parts + peers + gathers:
+        copy.wait_send()
+    finish_sends(spills)
+
+
+def close_kernel(ext, total, inverse, whole, probe, refined, new_probe):
+    win = ext.shape[3]
+    tile = ext.shape[2] - win
     for strip in range(2):
         for plane in range(2):
             refined[plane, :, strip * win : (strip + 1) * win] = (
                 ext[plane, strip, :tile] + total[plane, strip] * inverse[strip]
             )
-    for copy in gathers:
-        copy.wait_recv()
     value = whole[...]
     power = jnp.sum(value * value, axis=(0, 1), keepdims=True) / (value.shape[0] // 2 * win)
     new_probe[...] = probe[...] + value * lax.rsqrt(power + 1e-06)
-    for copy in parts + peers + gathers:
-        copy.wait_send()
-    finish_sends(spills)
 
 
 def remote_call(kernel, ident, out_shape, scratch, operands):
@@ -423,7 +429,9 @@
         in_specs=[vmem] * len(operands),
         out_specs=[vmem] * len(out_shape),
         scratch_shapes=scratch,
-        compiler_params=pltpu.CompilerParams(collective_id=ident, has_side_effects=True),
+        compiler_params=pltpu.CompilerParams(
+            collective_id=ident, has_side_effects=True, vmem_limit_bytes=GRANT
+        ),
     )(*operands)
 
 
@@ -463,32 +471,31 @@
     spread, *spills, gradient, narrow = sweep(False, corners, live, ext, probe, amp, ahead, back)
     flat = (2 * win, win)
     height = 2 * win // rows
-    refined, new_probe = remote_call(
+    total, whole = remote_call(
         functools.partial(last_kernel, rows, cols),
         2,
-        [jax.ShapeDtypeStruct(object_field.shape, f32), jax.ShapeDtypeStruct(flat, f32)],
+        [jax.ShapeDtypeStruct((2, 2, tile, win), f32), jax.ShapeDtypeStruct(flat, f32)],
         boxes(2)
         + [
-            pltpu.VMEM((2, 2, tile, win), f32),
             pltpu.VMEM((rows - 1, height, win), b16),
             pltpu.VMEM((cols, height, win), b16),
-            pltpu.VMEM(flat, f32),
             pltpu.VMEM((height, win), b16),
             sem((2, 3)),
             sem((2, rows - 1)),
             sem((2, cols - 1)),
             sem((2, rows - 1)),
         ],
-        [
-            spread,
-            *spills,
-            ext,
-            inverse,
-            gradient.reshape(flat),
-            narrow.reshape(flat),
-            probe.reshape(flat),
-        ],
-    )
+        [spread, *spills, gradient.reshape(flat), narrow.reshape(flat)],
+    )
+    vmem = pl.BlockSpec(memory_space=pltpu.VMEM)
+    refined, new_probe = pl.pallas_call(
+        close_kernel,
+        out_shape=[jax.ShapeDtypeStruct(object_field.shape, f32), jax.ShapeDtypeStruct(flat, f32)],
+        in_specs=[vmem] * 5,
+        out_specs=[vmem] * 2,
+        compiler_params=pltpu.CompilerParams(vmem_limit_bytes=GRANT),
+        name="close",
+    )(ext, total, inverse, whole, probe.reshape(flat))
     return (refined, new_probe.reshape(probe.shape))
 
 

time: 64.7 us -> 51.6 us (0.80); the launches traced: 65.1 us -> 51 us
  Pallas kernels: 60.3 us -> 48.5 us
  local copies, waits for them, and re-layouts: 3.44 us -> 1.05 us
    pallas_call x3, Pallas kernels: 49.9 us -> 41.6 us  [remote_call(): pl.pallas_call(kernel, out_shape=out_shape, in_specs=[vmem] * len(operand...]
    pallas_call x2, Pallas kernels: 10.4 us -> 6.01 us  [sweep(): pl.pallas_call(functools.partial(sweep_kernel, with_light), out_shape=out...]
    unnamed x2 -> x12, local copies, waits for them, and re-layouts: 3.44 us -> 1.05 us
    pallas_call x0 -> x1, Pallas kernels: none -> 0.92 us  [on_device(): pl.pallas_call(close_kernel, out_shape=[jax.ShapeDtypeStruct(object_field...]
where the time goes in v4:
time: 51.6 us; the launch traced here: 51 us
  Pallas kernels  48.5 us (94%)
  between operations  1.39 us (3%)
  local copies, waits for them, and re-layouts  1.05 us (2%)
    pallas_call x3, Pallas kernels, remote_call(): pl.pallas_call(kernel, out_shape=out_shape, in_specs=[vmem] * len(operand...  41.6 us
    pallas_call x2, Pallas kernels, sweep(): pl.pallas_call(functools.partial(sweep_kernel, with_light), out_shape=out...  6.01 us
    unnamed x12, local copies, waits for them, and re-layouts  1.05 us

profile of v4, /device:TPU:0, one launch (start us, length us, event | category | flops | bytes accessed | tf_op | source)
XLA Modules:
  0.0 51.0 jit_solution(4982616674375915055)
XLA Ops:
  0.6 0.0 copy-start.5
  1.3 0.0 copy-start
  1.3 1.0 %copy-done = f32[2,256,256]{2,1,0:T(8,128)S(1)} copy-done((f32[2,256,256]{2,1,0:T(8,128)S(1)}, f32[2,256,256]{2,1,0:T(8,128)}, u32[]{:S(2)}) %copy-start) | copy-done | bytes 524312
  2.3 0.0 copy-start.1
  2.3 0.0 copy-start.2
  2.3 0.0 copy-start.3
  2.3 0.0 copy-start.4
  2.4 10.4 %shard_map.86.ext = f32[2,3,384,128]{3,2,1,0:T(8,128)S(1)} custom-call(f32[2,256,256]{2,1,0:T(8,128)S(1)} %copy-done), custom_call_target="tpu_custom_call" | custom-call | tf_op jit(solution)/shard_map/pallas_call | solution.py:426
  12.7 0.0 copy-done.5
  12.7 0.0 copy-done.1
  12.7 0.0 copy-done.2
  12.8 0.0 copy-done.3
  12.8 0.0 copy-done.4
  12.8 3.0 %first_sweep.1 = (f32[3,3,384,128]{3,2,1,0:T(8,128)S(1)}, bf16[3,256,128]{2,1,0:T(8,128)(2,1)S(1)}, bf16[3,2,128,128]{3,2,1,0:T(8,128)(2,1)S(1)}, bf16[3,128,128]{2,1,0:T(8,128)(2,1)S(1)}) custom-call(s32[2,16]{1,0:T(2,128)S(1)} %bitcast.14, s32[1]{0:T(128)} %bitcast.7.live, f32[2,3,384,128]{3,2,1,0:T(8,128)S(1)} %shard_map.86.ext, ...), custom_call_target="tpu_custom_call" | custom-call | tf_op jit(solution)/shard_map/first_sweep/pallas_call | solution.py:142
  15.8 13.8 %shard_map.87 = (f32[2,3,384,128]{3,2,1,0:T(8,128)S(1)}, f32[2,256,128]{2,1,0:T(8,128)S(1)}) custom-call(f32[3,3,384,128]{3,2,1,0:T(8,128)S(1)} %get-tuple-element.18.refs_0_, bf16[3,256,128]{2,1,0:T(8,128)(2,1)S(1)} %get-tuple-element.19.refs_1_, bf16[3,2,128,128]{3,2,1,0:T(8,128)(2,1)S(1)} %get-tuple-element.20.refs_2_, ...), custom_call_target="tpu_custom_call" | custom-call | tf_op jit(solution)/shard_map/pallas_call | solution.py:426
  29.6 3.0 %second_sweep.1 = (f32[2,3,384,128]{3,2,1,0:T(8,128)S(1)}, bf16[2,256,128]{2,1,0:T(8,128)(2,1)S(1)}, bf16[2,2,128,128]{3,2,1,0:T(8,128)(2,1)S(1)}, bf16[2,128,12...) custom-call(s32[2,16]{1,0:T(2,128)S(1)} %bitcast.15, s32[1]{0:T(128)} %bitcast.8.live, ...), custom_call_target="tpu_custom_call" | custom-call | tf_op jit(solution)/shard_map/second_sweep/pallas_call | solution.py:142
  32.6 17.4 %shard_map.88 = (f32[2,2,256,128]{3,2,1,0:T(8,128)S(1)}, f32[256,128]{1,0:T(8,128)S(1)}) custom-call(f32[2,3,384,128]{3,2,1,0:T(8,128)S(1)} %get-tuple-element.23.refs_0_, bf16[2,256,128]{2,1,0:T(8,128)(2,1)S(1)} %get-tuple-element.24.refs_1_, bf16[2,2,128,128]{3,2,1,0:T(8,128)(2,1)S(1)} %get-tuple-element.25.refs_2_, ...), custom_call_target="tpu_custom_call" | custom-call | tf_op jit(solution)/shard_map/pallas_call | solution.py:426
  50.0 0.9 %close.1 = (f32[2,256,256]{2,1,0:T(8,128)}, f32[256,128]{1,0:T(8,128)}) custom-call(f32[2,3,384,128]{3,2,1,0:T(8,128)S(1)} %get-tuple-element.22.ext, f32[2,2,256,128]{3,2,1,0:T(8,128)S(1)} %get-tuple-element.29.total, f32[2,256,128]{2,1,0:T(8,128)S(1)} %get-tuple-element.30.inverse, f32[256,128]{1,0:T(8,128)S(1)} %get-tuple-element.31.whole, ...), custom_call_target="tpu_custom_call" | custom-call | tf_op jit(solution)/shard_map/close/pallas_call | solution.py:491
Async XLA Ops:
  0.6 12.1 %copy-start.5 = (s32[2,1,1,16]{3,2,1,0:T(1,128)S(1)}, s32[2,1,1,16]{3,2,1,0:T(1,128)}, u32[]{:S(2)}) copy-start(s32[2,1,1,16]{3,2,1,0:T(1,128)} %param.10) | copy-start | bytes 388
  1.3 1.0 %copy-start = (f32[2,256,256]{2,1,0:T(8,128)S(1)}, f32[2,256,256]{2,1,0:T(8,128)}, u32[]{:S(2)}) copy-start(f32[2,256,256]{2,1,0:T(8,128)} %refs_4_.1) | copy-start | bytes 1572868
  2.3 10.4 %copy-start.1 = (bf16[1,1,16,128,128]{4,3,2,1,0:T(8,128)(2,1)S(1)}, bf16[1,1,16,128,128]{4,3,2,1,0:T(8,128)(2,1)}, u32[]{:S(2)}) copy-start(bf16[1,1,16,128,128]{4,3,2,1,0:T(8,128)(2,1)} %param.9) | copy-start | bytes 1572868
  2.3 10.4 %copy-start.2 = (f32[2,128,128]{2,1,0:T(8,128)S(1)}, f32[2,128,128]{2,1,0:T(8,128)}, u32[]{:S(2)}) copy-start(f32[2,128,128]{2,1,0:T(8,128)} %probe.3) | copy-start | bytes 393220
  2.3 10.4 %copy-start.3 = (bf16[256,256]{1,0:T(8,128)(2,1)S(1)}, bf16[256,256]{1,0:T(8,128)(2,1)}, u32[]{:S(2)}) copy-start(bf16[256,256]{1,0:T(8,128)(2,1)} %constant.5.clone.back) | copy-start | bytes 393220
  2.3 10.4 %copy-start.4 = (bf16[256,256]{1,0:T(8,128)(2,1)S(1)}, bf16[256,256]{1,0:T(8,128)(2,1)}, u32[]{:S(2)}) copy-start(bf16[256,256]{1,0:T(8,128)(2,1)} %constant.4.clone.ahead) | copy-start | bytes 393220

commit v5 on v4

--- a/solution.py
+++ b/solution.py
@@ -9,7 +9,7 @@
 from jax.experimental.pallas import tpu as pltpu
 from jax.sharding import PartitionSpec as P
 
-GROUP = 4
+GROUP = 8
 GRANT = 12 << 20
 
 
@@ -190,6 +190,7 @@
     pl.semaphore_wait(barrier, others)
 
 
+NEXT = ((0, -1), (-1, 0), (0, 1), (1, 0))
 NEAR = ((0, -1), (-1, 0), (-1, -1), (0, 1), (1, 0), (1, 1))
 
 
@@ -238,17 +239,28 @@
 def fill_rims(shifts, ext, side_in, low_in, corner_in):
     win = ext.shape[3]
     tile = ext.shape[2] - win
-
-    def low():
+    top, bottom, low, onward = shifts
+
+    @pl.when(top.receives)
+    def _():
+        top.copy.wait_recv()
+
+    onward.start()
+
+    @pl.when(low.receives)
+    def _():
+        low.copy.wait_recv()
         ext[:, :2, tile:] = low_in[...].astype(jnp.float32)
 
-    def side():
+    @pl.when(bottom.receives)
+    def _():
+        bottom.copy.wait_recv()
         ext[:, 2, :tile] = side_in[...].astype(jnp.float32)
 
-    def corner():
+    @pl.when(onward.receives)
+    def _():
+        onward.copy.wait_recv()
         ext[:, 2, tile:] = corner_in[...].astype(jnp.float32)
-
-    arrive(shifts, side, low, corner)
 
 
 def add_spills(shifts, total, side_in, low_in, corner_in):
@@ -269,27 +281,30 @@
 def rim_boxes(place, outs, ins, win, sems):
     side_out, low_out = outs
     side_in, low_in, corner_in = ins
-    return box_shifts(
-        place,
-        -1,
-        (side_out, side_in),
-        (low_out, low_in),
-        (side_out.at[:, pl.ds(0, win)], corner_in),
-        sems,
-    )
+    top, bottom = pl.ds(0, win), pl.ds(win, side_in.shape[1] - win)
+    left = (0, -1)
+    onward = Shift(place, (-1, 0), side_in.at[:, top], corner_in, sems, 3)
+    onward.sends = place.inside(-1, 1)
+    onward.receives = place.inside(1, 1)
+    return [
+        Shift(place, left, side_out.at[:, top], side_in.at[:, top], sems, 0),
+        Shift(place, left, side_out.at[:, bottom], side_in.at[:, bottom], sems, 1),
+        Shift(place, (-1, 0), low_out, low_in, sems, 2),
+        onward,
+    ]
 
 
 def extend_kernel(rows, cols, obj, ext, side_out, low_out, side_in, low_in, corner_in, sems):
     win = ext.shape[3]
     tile = ext.shape[2] - win
     place = Place(rows, cols)
-    barrier = greet(place, NEAR)
+    barrier = greet(place, NEXT)
     side_out[...] = obj[:, :, :win].astype(jnp.bfloat16)
     for strip in range(2):
         low_out[:, strip] = obj[:, :win, strip * win : (strip + 1) * win].astype(jnp.bfloat16)
-    meet(place, barrier, NEAR)
+    meet(place, barrier, NEXT)
     shifts = rim_boxes(place, (side_out, low_out), (side_in, low_in, corner_in), win, sems)
-    for shift in shifts:
+    for shift in shifts[:3]:
         shift.start()
     for strip in range(2):
         ext[:, strip, :tile] = obj[:, :, strip * win : (strip + 1) * win]
@@ -328,7 +343,7 @@
             low_out[plane, strip] = fresh[:win].astype(jnp.bfloat16)
             ext[plane, strip, :tile] = fresh
         inverse[strip] = share
-        for rim in rims[:2] if strip == 0 else rims[2:]:
+        for rim in rims[:2] if strip == 0 else rims[2:3]:
             rim.start()
     finish_sends(spills)
     fill_rims(rims, ext, side_in, low_in, corner_in)
@@ -454,7 +469,7 @@
         functools.partial(extend_kernel, rows, cols),
         0,
         [ext_shape],
-        boxes(2, 2) + boxes(2) + [sem((2, 3))],
+        boxes(2, 2) + boxes(2) + [sem((2, 4))],
         [object_field],
     )
     spread, *spills = sweep(True, corners, live, ext, probe, amp, ahead, back)
@@ -465,7 +480,7 @@
         boxes(3)
         + boxes(2, 2)
         + boxes(2)
-        + [pltpu.VMEM((3, 2, tile, win), f32), sem((2, 3)), sem((2, 3))],
+        + [pltpu.VMEM((3, 2, tile, win), f32), sem((2, 3)), sem((2, 4))],
         [spread, *spills, object_field],
     )
     spread, *spills, gradient, narrow = sweep(False, corners, live, ext, probe, amp, ahead, back)

time: 51.6 us -> 50.9 us (0.986)
    pallas_call x3, Pallas kernels: 41.6 us -> 39.6 us  [remote_call(): pl.pallas_call(kernel, out_shape=out_shape, in_specs=[vmem] * len(operand...]
    pallas_call x2, Pallas kernels: 6.01 us -> 7.79 us  [sweep(): pl.pallas_call(functools.partial(sweep_kernel, with_light), out_shape=out...]
where the time goes in v5:
time: 50.9 us; the launch traced here: 50.8 us
  Pallas kernels  48.3 us (95%)
  between operations  1.39 us (3%)
  local copies, waits for them, and re-layouts  1.05 us (2%)
    pallas_call x3, Pallas kernels, remote_call(): pl.pallas_call(kernel, out_shape=out_shape, in_specs=[vmem] * len(operand...  39.6 us
    pallas_call x2, Pallas kernels, sweep(): pl.pallas_call(functools.partial(sweep_kernel, with_light), out_shape=out...  7.79 us
    unnamed x12, local copies, waits for them, and re-layouts  1.05 us

profile of v5, /device:TPU:0, one launch (start us, length us, event | category | flops | bytes accessed | tf_op | source)
XLA Modules:
  0.0 50.8 jit_solution(8291666772621927108)
XLA Ops:
  0.6 0.0 copy-start.5
  1.3 0.0 copy-start
  1.3 1.0 %copy-done = f32[2,256,256]{2,1,0:T(8,128)S(1)} copy-done((f32[2,256,256]{2,1,0:T(8,128)S(1)}, f32[2,256,256]{2,1,0:T(8,128)}, u32[]{:S(2)}) %copy-start) | copy-done | bytes 524312
  2.3 0.0 copy-start.1
  2.3 0.0 copy-start.2
  2.3 0.0 copy-start.3
  2.3 0.0 copy-start.4
  2.4 8.4 %shard_map.86.ext = f32[2,3,384,128]{3,2,1,0:T(8,128)S(1)} custom-call(f32[2,256,256]{2,1,0:T(8,128)S(1)} %copy-done), custom_call_target="tpu_custom_call" | custom-call | tf_op jit(solution)/shard_map/pallas_call | solution.py:441
  10.8 0.0 copy-done.5
  10.8 0.0 copy-done.1
  10.8 0.0 copy-done.2
  10.8 0.0 copy-done.3
  10.8 0.0 copy-done.4
  10.8 3.9 %first_sweep.1 = (f32[3,3,384,128]{3,2,1,0:T(8,128)S(1)}, bf16[3,256,128]{2,1,0:T(8,128)(2,1)S(1)}, bf16[3,2,128,128]{3,2,1,0:T(8,128)(2,1)S(1)}, bf16[3,128,128]{2,1,0:T(8,128)(2,1)S(1)}) custom-call(s32[2,16]{1,0:T(2,128)S(1)} %bitcast.14, s32[1]{0:T(128)} %bitcast.7.live, f32[2,3,384,128]{3,2,1,0:T(8,128)S(1)} %shard_map.86.ext, ...), custom_call_target="tpu_custom_call" | custom-call | tf_op jit(solution)/shard_map/first_sweep/pallas_call | solution.py:142
  14.7 13.8 %shard_map.87 = (f32[2,3,384,128]{3,2,1,0:T(8,128)S(1)}, f32[2,256,128]{2,1,0:T(8,128)S(1)}) custom-call(f32[3,3,384,128]{3,2,1,0:T(8,128)S(1)} %get-tuple-element.18.refs_0_, bf16[3,256,128]{2,1,0:T(8,128)(2,1)S(1)} %get-tuple-element.19.refs_1_, bf16[3,2,128,128]{3,2,1,0:T(8,128)(2,1)S(1)} %get-tuple-element.20.refs_2_, ...), custom_call_target="tpu_custom_call" | custom-call | tf_op jit(solution)/shard_map/pallas_call | solution.py:441
  28.5 3.9 %second_sweep.1 = (f32[2,3,384,128]{3,2,1,0:T(8,128)S(1)}, bf16[2,256,128]{2,1,0:T(8,128)(2,1)S(1)}, bf16[2,2,128,128]{3,2,1,0:T(8,128)(2,1)S(1)}, bf16[2,128,12...) custom-call(s32[2,16]{1,0:T(2,128)S(1)} %bitcast.15, s32[1]{0:T(128)} %bitcast.8.live, ...), custom_call_target="tpu_custom_call" | custom-call | tf_op jit(solution)/shard_map/second_sweep/pallas_call | solution.py:142
  32.4 17.5 %shard_map.88 = (f32[2,2,256,128]{3,2,1,0:T(8,128)S(1)}, f32[256,128]{1,0:T(8,128)S(1)}) custom-call(f32[2,3,384,128]{3,2,1,0:T(8,128)S(1)} %get-tuple-element.23.refs_0_, bf16[2,256,128]{2,1,0:T(8,128)(2,1)S(1)} %get-tuple-element.24.refs_1_, bf16[2,2,128,128]{3,2,1,0:T(8,128)(2,1)S(1)} %get-tuple-element.25.refs_2_, ...), custom_call_target="tpu_custom_call" | custom-call | tf_op jit(solution)/shard_map/pallas_call | solution.py:441
  49.9 0.9 %close.1 = (f32[2,256,256]{2,1,0:T(8,128)}, f32[256,128]{1,0:T(8,128)}) custom-call(f32[2,3,384,128]{3,2,1,0:T(8,128)S(1)} %get-tuple-element.22.ext, f32[2,2,256,128]{3,2,1,0:T(8,128)S(1)} %get-tuple-element.29.total, f32[2,256,128]{2,1,0:T(8,128)S(1)} %get-tuple-element.30.inverse, f32[256,128]{1,0:T(8,128)S(1)} %get-tuple-element.31.whole, ...), custom_call_target="tpu_custom_call" | custom-call | tf_op jit(solution)/shard_map/close/pallas_call | solution.py:506
Async XLA Ops:
  0.6 10.1 %copy-start.5 = (s32[2,1,1,16]{3,2,1,0:T(1,128)S(1)}, s32[2,1,1,16]{3,2,1,0:T(1,128)}, u32[]{:S(2)}) copy-start(s32[2,1,1,16]{3,2,1,0:T(1,128)} %param.10) | copy-start | bytes 388
  1.3 1.0 %copy-start = (f32[2,256,256]{2,1,0:T(8,128)S(1)}, f32[2,256,256]{2,1,0:T(8,128)}, u32[]{:S(2)}) copy-start(f32[2,256,256]{2,1,0:T(8,128)} %refs_4_.1) | copy-start | bytes 1572868
  2.3 8.4 %copy-start.1 = (bf16[1,1,16,128,128]{4,3,2,1,0:T(8,128)(2,1)S(1)}, bf16[1,1,16,128,128]{4,3,2,1,0:T(8,128)(2,1)}, u32[]{:S(2)}) copy-start(bf16[1,1,16,128,128]{4,3,2,1,0:T(8,128)(2,1)} %param.9) | copy-start | bytes 1572868
  2.3 8.4 %copy-start.2 = (f32[2,128,128]{2,1,0:T(8,128)S(1)}, f32[2,128,128]{2,1,0:T(8,128)}, u32[]{:S(2)}) copy-start(f32[2,128,128]{2,1,0:T(8,128)} %probe.3) | copy-start | bytes 393220
  2.3 8.5 %copy-start.3 = (bf16[256,256]{1,0:T(8,128)(2,1)S(1)}, bf16[256,256]{1,0:T(8,128)(2,1)}, u32[]{:S(2)}) copy-start(bf16[256,256]{1,0:T(8,128)(2,1)} %constant.5.clone.back) | copy-start | bytes 393220
  2.3 8.5 %copy-start.4 = (bf16[256,256]{1,0:T(8,128)(2,1)S(1)}, bf16[256,256]{1,0:T(8,128)(2,1)}, u32[]{:S(2)}) copy-start(bf16[256,256]{1,0:T(8,128)(2,1)} %constant.4.clone.ahead) | copy-start | bytes 393220

commit v6 on v5

--- a/solution.py
+++ b/solution.py
@@ -191,7 +191,6 @@
 
 
 NEXT = ((0, -1), (-1, 0), (0, 1), (1, 0))
-NEAR = ((0, -1), (-1, 0), (-1, -1), (0, 1), (1, 0), (1, 1))
 
 
 class Shift:
@@ -214,26 +213,41 @@
         pl.when(self.sends)(self.copy.wait_send)
 
 
-def box_shifts(place, down, side, low, corner, sems):
+def spill_shifts(place, spills, got, mixed, sems):
+    side, low, corner = spills
+    side_got, low_got, corner_got = got
+    win = corner.shape[1]
+    top, bottom = pl.ds(0, win), pl.ds(win, side.shape[1] - win)
+    below = Shift(place, (1, 0), corner, corner_got, sems, 0)
+    below.sends = place.inside(1, 1)
+    below.receives = place.inside(-1, 1)
     return [
-        Shift(place, (0, down), *side, sems, 0),
-        Shift(place, (down, down), *corner, sems, 1),
-        Shift(place, (down, 0), *low, sems, 2),
+        below,
+        Shift(place, (0, 1), side.at[:, bottom], side_got.at[:, bottom], sems, 1),
+        Shift(place, (1, 0), low, low_got, sems, 2),
+        Shift(place, (0, 1), mixed, side_got.at[:, top], sems, 3),
     ]
+
+
+def pass_corner(shifts, spread, side, corner_got, mixed):
+    win = corner_got.shape[1]
+    below = shifts[0]
+
+    @pl.when(below.receives)
+    def _():
+        below.copy.wait_recv()
+        mixed[...] = (spread[:, 2, :win] + corner_got[...].astype(jnp.float32)).astype(jnp.bfloat16)
+
+    @pl.when(jnp.logical_not(below.receives))
+    def _():
+        mixed[...] = side[:, :win]
+
+    shifts[3].start()
 
 
 def finish_sends(shifts):
     for shift in shifts:
         shift.wait_send()
-
-
-def arrive(shifts, side, low, corner):
-    for shift, action in zip((shifts[2], shifts[0], shifts[1]), (low, side, corner)):
-
-        @pl.when(shift.receives)
-        def _():
-            shift.copy.wait_recv()
-            action()
 
 
 def fill_rims(shifts, ext, side_in, low_in, corner_in):
@@ -263,19 +277,25 @@
         ext[:, 2, tile:] = corner_in[...].astype(jnp.float32)
 
 
-def add_spills(shifts, total, side_in, low_in, corner_in):
+def add_spills(shifts, total, got):
+    side_got, low_got, corner_got = got
     win = total.shape[3]
-
-    def low():
-        total[:, :, :win] += low_in[...].astype(jnp.float32)
-
-    def side():
-        total[:, 0] += side_in[...].astype(jnp.float32)
-
-    def corner():
-        total[:, 0, :win] += corner_in[...].astype(jnp.float32)
-
-    arrive(shifts, side, low, corner)
+    below, bottom, low, top = shifts
+
+    @pl.when(low.receives)
+    def _():
+        low.copy.wait_recv()
+        total[:, :, :win] += low_got[...].astype(jnp.float32)
+
+    @pl.when(bottom.receives)
+    def _():
+        bottom.copy.wait_recv()
+        total[:, 0, win:] += side_got[:, win:].astype(jnp.float32)
+
+    @pl.when(top.receives)
+    def _():
+        top.copy.wait_recv()
+        total[:, 0, :win] += side_got[:, :win].astype(jnp.float32)
 
 
 def rim_boxes(place, outs, ins, win, sems):
@@ -314,25 +334,20 @@
 
 def update_kernel(rows, cols, *refs):
     spread, side_spill, low_spill, corner_spill, obj, ext, inverse = refs[:7]
-    side_got, low_got, corner_got, side_out, low_out, side_in, low_in, corner_in = refs[7:15]
-    total, sems, rim_sems = refs[15:]
+    got = refs[7:10]
+    side_out, low_out, side_in, low_in, corner_in = refs[10:15]
+    total, mixed, sems, rim_sems = refs[15:]
     win = ext.shape[3]
     tile = ext.shape[2] - win
     place = Place(rows, cols)
-    barrier = greet(place, NEAR)
-    meet(place, barrier, NEAR)
-    spills = box_shifts(
-        place,
-        1,
-        (side_spill, side_got),
-        (low_spill, low_got),
-        (corner_spill, corner_got),
-        sems,
-    )
-    for shift in spills:
+    barrier = greet(place, NEXT)
+    meet(place, barrier, NEXT)
+    spills = spill_shifts(place, (side_spill, low_spill, corner_spill), got, mixed, sems)
+    for shift in spills[:3]:
         shift.start()
     total[...] = spread[:, :2, :tile]
-    add_spills(spills, total, side_got, low_got, corner_got)
+    pass_corner(spills, spread, side_spill, got[2], mixed)
+    add_spills(spills, total, got)
     rims = rim_boxes(place, (side_out, low_out), (side_in, low_in, corner_in), win, rim_sems)
     for strip in range(2):
         share = 1.0 / (total[2, strip] + 4.0)
@@ -352,17 +367,17 @@
 
 def last_kernel(rows, cols, *refs):
     spread, side_spill, low_spill, corner_spill, gradient, narrow = refs[:6]
-    total, whole, side_got, low_got, corner_got = refs[6:11]
-    part_in, peer_in, own, sems, part_sems, peer_sems, whole_sems = refs[11:]
+    total, whole = refs[6:8]
+    got, mixed = refs[8:11], refs[11]
+    part_in, peer_in, own, sems, part_sems, peer_sems, whole_sems = refs[12:]
     tile = total.shape[2]
     place = Place(rows, cols)
-    diagonal = ((-1, -1), (1, 1))
-    barrier = greet(place, diagonal)
+    barrier = pltpu.get_barrier_semaphore()
     col_peers = [place.at(0, step) for step in range(1, cols)]
     row_peers = [place.at(step, 0) for step in range(1, rows)]
     for peer in col_peers + row_peers:
         pl.semaphore_signal(barrier, inc=1, device_id=peer, device_id_type=MESH)
-    meet(place, barrier, diagonal, cols + rows - 2)
+    pl.semaphore_wait(barrier, cols + rows - 2)
     height = whole.shape[0] // rows
 
     def piece(index):
@@ -384,15 +399,8 @@
         send(narrow.at[piece(peer[0])], part_in.at[index], part_sems, index, peer)
         for index, peer in enumerate(row_peers)
     ]
-    spills = box_shifts(
-        place,
-        1,
-        (side_spill, side_got),
-        (low_spill, low_got),
-        (corner_spill, corner_got),
-        sems,
-    )
-    for shift in spills:
+    spills = spill_shifts(place, (side_spill, low_spill, corner_spill), got, mixed, sems)
+    for shift in spills[:3]:
         shift.start()
     summed = gradient[piece(place.row)]
     for index, copy in enumerate(parts):
@@ -404,6 +412,7 @@
         send(own, peer_in.at[place.col], peer_sems, index, peer)
         for index, peer in enumerate(col_peers)
     ]
+    pass_corner(spills, spread, side_spill, got[2], mixed)
     total[...] = spread[:, :2, :tile]
     for copy in peers:
         copy.wait_recv()
@@ -415,7 +424,7 @@
         send(whole.at[piece(place.row)], whole.at[piece(place.row)], whole_sems, index, peer)
         for index, peer in enumerate(row_peers)
     ]
-    add_spills(spills, total, side_got, low_got, corner_got)
+    add_spills(spills, total, got)
     for copy in gathers:
         copy.wait_recv()
     for copy in parts + peers + gathers:
@@ -480,7 +489,12 @@
         boxes(3)
         + boxes(2, 2)
         + boxes(2)
-        + [pltpu.VMEM((3, 2, tile, win), f32), sem((2, 3)), sem((2, 4))],
+        + [
+            pltpu.VMEM((3, 2, tile, win), f32),
+            pltpu.VMEM((3, win, win), b16),
+            sem((2, 4)),
+            sem((2, 4)),
+        ],
         [spread, *spills, object_field],
     )
     spread, *spills, gradient, narrow = sweep(False, corners, live, ext, probe, amp, ahead, back)
@@ -492,10 +506,11 @@
         [jax.ShapeDtypeStruct((2, 2, tile, win), f32), jax.ShapeDtypeStruct(flat, f32)],
         boxes(2)
         + [
+            pltpu.VMEM((2, win, win), b16),
             pltpu.VMEM((rows - 1, height, win), b16),
             pltpu.VMEM((cols, height, win), b16),
             pltpu.VMEM((height, win), b16),
-            sem((2, 3)),
+            sem((2, 4)),
             sem((2, rows - 1)),
             sem((2, cols - 1)),
             sem((2, rows - 1)),

time: 50.9 us -> 49.5 us (0.972)
  Pallas kernels: 48.3 us -> 46.5 us
    pallas_call x3, Pallas kernels: 39.6 us -> 37.8 us  [remote_call(): pl.pallas_call(kernel, out_shape=out_shape, in_specs=[vmem] * len(operand...]
where the time goes in v6:
time: 49.5 us; the launch traced here: 48.9 us
  Pallas kernels  46.5 us (94%)
  between operations  1.39 us (3%)
  local copies, waits for them, and re-layouts  1.05 us (2%)
    pallas_call x3, Pallas kernels, remote_call(): pl.pallas_call(kernel, out_shape=out_shape, in_specs=[vmem] * len(operand...  37.8 us
    pallas_call x2, Pallas kernels, sweep(): pl.pallas_call(functools.partial(sweep_kernel, with_light), out_shape=out...  7.75 us
    unnamed x12, local copies, waits for them, and re-layouts  1.05 us

profile of v6, /device:TPU:0, one launch (start us, length us, event | category | flops | bytes accessed | tf_op | source)
XLA Modules:
  0.0 48.9 jit_solution(4250268269149216248)
XLA Ops:
  0.6 0.0 copy-start.5
  1.3 0.0 copy-start
  1.3 1.0 %copy-done = f32[2,256,256]{2,1,0:T(8,128)S(1)} copy-done((f32[2,256,256]{2,1,0:T(8,128)S(1)}, f32[2,256,256]{2,1,0:T(8,128)}, u32[]{:S(2)}) %copy-start) | copy-done | bytes 524312
  2.3 0.0 copy-start.1
  2.3 0.0 copy-start.2
  2.3 0.0 copy-start.3
  2.3 0.0 copy-start.4
  2.4 8.4 %shard_map.86.ext = f32[2,3,384,128]{3,2,1,0:T(8,128)S(1)} custom-call(f32[2,256,256]{2,1,0:T(8,128)S(1)} %copy-done), custom_call_target="tpu_custom_call" | custom-call | tf_op jit(solution)/shard_map/pallas_call | solution.py:450
  10.8 0.0 copy-done.5
  10.8 0.0 copy-done.1
  10.8 0.0 copy-done.2
  10.8 0.0 copy-done.3
  10.8 0.0 copy-done.4
  10.8 3.8 %first_sweep.1 = (f32[3,3,384,128]{3,2,1,0:T(8,128)S(1)}, bf16[3,256,128]{2,1,0:T(8,128)(2,1)S(1)}, bf16[3,2,128,128]{3,2,1,0:T(8,128)(2,1)S(1)}, bf16[3,128,128]{2,1,0:T(8,128)(2,1)S(1)}) custom-call(s32[2,16]{1,0:T(2,128)S(1)} %bitcast.14, s32[1]{0:T(128)} %bitcast.7.live, f32[2,3,384,128]{3,2,1,0:T(8,128)S(1)} %shard_map.86.ext, ...), custom_call_target="tpu_custom_call" | custom-call | tf_op jit(solution)/shard_map/first_sweep/pallas_call | solution.py:142
  14.7 12.3 %shard_map.87 = (f32[2,3,384,128]{3,2,1,0:T(8,128)S(1)}, f32[2,256,128]{2,1,0:T(8,128)S(1)}) custom-call(f32[3,3,384,128]{3,2,1,0:T(8,128)S(1)} %get-tuple-element.18.refs_0_, bf16[3,256,128]{2,1,0:T(8,128)(2,1)S(1)} %get-tuple-element.19.refs_1_, bf16[3,2,128,128]{3,2,1,0:T(8,128)(2,1)S(1)} %get-tuple-element.20.refs_2_, ...), custom_call_target="tpu_custom_call" | custom-call | tf_op jit(solution)/shard_map/pallas_call | solution.py:450
  26.9 3.9 %second_sweep.1 = (f32[2,3,384,128]{3,2,1,0:T(8,128)S(1)}, bf16[2,256,128]{2,1,0:T(8,128)(2,1)S(1)}, bf16[2,2,128,128]{3,2,1,0:T(8,128)(2,1)S(1)}, bf16[2,128,12...) custom-call(s32[2,16]{1,0:T(2,128)S(1)} %bitcast.15, s32[1]{0:T(128)} %bitcast.8.live, ...), custom_call_target="tpu_custom_call" | custom-call | tf_op jit(solution)/shard_map/second_sweep/pallas_call | solution.py:142
  30.8 17.2 %shard_map.88 = (f32[2,2,256,128]{3,2,1,0:T(8,128)S(1)}, f32[256,128]{1,0:T(8,128)S(1)}) custom-call(f32[2,3,384,128]{3,2,1,0:T(8,128)S(1)} %get-tuple-element.23.refs_0_, bf16[2,256,128]{2,1,0:T(8,128)(2,1)S(1)} %get-tuple-element.24.refs_1_, bf16[2,2,128,128]{3,2,1,0:T(8,128)(2,1)S(1)} %get-tuple-element.25.refs_2_, ...), custom_call_target="tpu_custom_call" | custom-call | tf_op jit(solution)/shard_map/pallas_call | solution.py:450
  48.0 0.9 %close.1 = (f32[2,256,256]{2,1,0:T(8,128)}, f32[256,128]{1,0:T(8,128)}) custom-call(f32[2,3,384,128]{3,2,1,0:T(8,128)S(1)} %get-tuple-element.22.ext, f32[2,2,256,128]{3,2,1,0:T(8,128)S(1)} %get-tuple-element.29.total, f32[2,256,128]{2,1,0:T(8,128)S(1)} %get-tuple-element.30.inverse, f32[256,128]{1,0:T(8,128)S(1)} %get-tuple-element.31.whole, ...), custom_call_target="tpu_custom_call" | custom-call | tf_op jit(solution)/shard_map/close/pallas_call | solution.py:521
Async XLA Ops:
  0.6 10.1 %copy-start.5 = (s32[2,1,1,16]{3,2,1,0:T(1,128)S(1)}, s32[2,1,1,16]{3,2,1,0:T(1,128)}, u32[]{:S(2)}) copy-start(s32[2,1,1,16]{3,2,1,0:T(1,128)} %param.10) | copy-start | bytes 388
  1.3 1.0 %copy-start = (f32[2,256,256]{2,1,0:T(8,128)S(1)}, f32[2,256,256]{2,1,0:T(8,128)}, u32[]{:S(2)}) copy-start(f32[2,256,256]{2,1,0:T(8,128)} %refs_4_.1) | copy-start | bytes 1572868
  2.3 8.4 %copy-start.1 = (bf16[1,1,16,128,128]{4,3,2,1,0:T(8,128)(2,1)S(1)}, bf16[1,1,16,128,128]{4,3,2,1,0:T(8,128)(2,1)}, u32[]{:S(2)}) copy-start(bf16[1,1,16,128,128]{4,3,2,1,0:T(8,128)(2,1)} %param.9) | copy-start | bytes 1572868
  2.3 8.4 %copy-start.2 = (f32[2,128,128]{2,1,0:T(8,128)S(1)}, f32[2,128,128]{2,1,0:T(8,128)}, u32[]{:S(2)}) copy-start(f32[2,128,128]{2,1,0:T(8,128)} %probe.3) | copy-start | bytes 393220
  2.3 8.5 %copy-start.3 = (bf16[256,256]{1,0:T(8,128)(2,1)S(1)}, bf16[256,256]{1,0:T(8,128)(2,1)}, u32[]{:S(2)}) copy-start(bf16[256,256]{1,0:T(8,128)(2,1)} %constant.5.clone.back) | copy-start | bytes 393220
  2.3 8.5 %copy-start.4 = (bf16[256,256]{1,0:T(8,128)(2,1)S(1)}, bf16[256,256]{1,0:T(8,128)(2,1)}, u32[]{:S(2)}) copy-start(bf16[256,256]{1,0:T(8,128)(2,1)} %constant.4.clone.ahead) | copy-start | bytes 393220

commit v7 on v6

--- a/solution.py
+++ b/solution.py
@@ -9,7 +9,7 @@
 from jax.experimental.pallas import tpu as pltpu
 from jax.sharding import PartitionSpec as P
 
-GROUP = 8
+GROUP = 16
 GRANT = 12 << 20
 
 

time: 49.5 us -> 48.8 us (0.986)
    pallas_call x2, Pallas kernels: 7.75 us -> 7.2 us  [sweep(): pl.pallas_call(functools.partial(sweep_kernel, with_light), out_shape=out...]
where the time goes in v7:
time: 48.8 us; the launch traced here: 48.6 us
  Pallas kernels  46.2 us (95%)
  between operations  1.39 us (3%)
  local copies, waits for them, and re-layouts  1.05 us (2%)
    pallas_call x3, Pallas kernels, remote_call(): pl.pallas_call(kernel, out_shape=out_shape, in_specs=[vmem] * len(operand...  38.1 us
    pallas_call x2, Pallas kernels, sweep(): pl.pallas_call(functools.partial(sweep_kernel, with_light), out_shape=out...  7.2 us
    unnamed x12, local copies, waits for them, and re-layouts  1.05 us

profile of v7, /device:TPU:0, one launch (start us, length us, event | category | flops | bytes accessed | tf_op | source)
XLA Modules:
  0.0 48.6 jit_solution(3120337754856183590)
XLA Ops:
  0.6 0.0 copy-start.5
  1.3 0.0 copy-start
  1.3 1.0 %copy-done = f32[2,256,256]{2,1,0:T(8,128)S(1)} copy-done((f32[2,256,256]{2,1,0:T(8,128)S(1)}, f32[2,256,256]{2,1,0:T(8,128)}, u32[]{:S(2)}) %copy-start) | copy-done | bytes 524312
  2.3 0.0 copy-start.1
  2.3 0.0 copy-start.2
  2.3 0.0 copy-start.3
  2.3 0.0 copy-start.4
  2.4 8.4 %shard_map.86.ext = f32[2,3,384,128]{3,2,1,0:T(8,128)S(1)} custom-call(f32[2,256,256]{2,1,0:T(8,128)S(1)} %copy-done), custom_call_target="tpu_custom_call" | custom-call | tf_op jit(solution)/shard_map/pallas_call | solution.py:450
  10.8 0.0 copy-done.5
  10.8 0.0 copy-done.1
  10.8 0.0 copy-done.2
  10.8 0.0 copy-done.3
  10.8 0.0 copy-done.4
  10.8 3.6 %first_sweep.1 = (f32[3,3,384,128]{3,2,1,0:T(8,128)S(1)}, bf16[3,256,128]{2,1,0:T(8,128)(2,1)S(1)}, bf16[3,2,128,128]{3,2,1,0:T(8,128)(2,1)S(1)}, bf16[3,128,128]{2,1,0:T(8,128)(2,1)S(1)}) custom-call(s32[2,16]{1,0:T(2,128)S(1)} %bitcast.14, s32[1]{0:T(128)} %bitcast.7.live, f32[2,3,384,128]{3,2,1,0:T(8,128)S(1)} %shard_map.86.ext, ...), custom_call_target="tpu_custom_call" | custom-call | tf_op jit(solution)/shard_map/first_sweep/pallas_call | solution.py:142
  14.4 13.9 %shard_map.87 = (f32[2,3,384,128]{3,2,1,0:T(8,128)S(1)}, f32[2,256,128]{2,1,0:T(8,128)S(1)}) custom-call(f32[3,3,384,128]{3,2,1,0:T(8,128)S(1)} %get-tuple-element.18.refs_0_, bf16[3,256,128]{2,1,0:T(8,128)(2,1)S(1)} %get-tuple-element.19.refs_1_, bf16[3,2,128,128]{3,2,1,0:T(8,128)(2,1)S(1)} %get-tuple-element.20.refs_2_, ...), custom_call_target="tpu_custom_call" | custom-call | tf_op jit(solution)/shard_map/pallas_call | solution.py:450
  28.3 3.6 %second_sweep.1 = (f32[2,3,384,128]{3,2,1,0:T(8,128)S(1)}, bf16[2,256,128]{2,1,0:T(8,128)(2,1)S(1)}, bf16[2,2,128,128]{3,2,1,0:T(8,128)(2,1)S(1)}, bf16[2,128,12...) custom-call(s32[2,16]{1,0:T(2,128)S(1)} %bitcast.15, s32[1]{0:T(128)} %bitcast.8.live, ...), custom_call_target="tpu_custom_call" | custom-call | tf_op jit(solution)/shard_map/second_sweep/pallas_call | solution.py:142
  31.9 15.8 %shard_map.88 = (f32[2,2,256,128]{3,2,1,0:T(8,128)S(1)}, f32[256,128]{1,0:T(8,128)S(1)}) custom-call(f32[2,3,384,128]{3,2,1,0:T(8,128)S(1)} %get-tuple-element.23.refs_0_, bf16[2,256,128]{2,1,0:T(8,128)(2,1)S(1)} %get-tuple-element.24.refs_1_, bf16[2,2,128,128]{3,2,1,0:T(8,128)(2,1)S(1)} %get-tuple-element.25.refs_2_, ...), custom_call_target="tpu_custom_call" | custom-call | tf_op jit(solution)/shard_map/pallas_call | solution.py:450
  47.7 0.9 %close.1 = (f32[2,256,256]{2,1,0:T(8,128)}, f32[256,128]{1,0:T(8,128)}) custom-call(f32[2,3,384,128]{3,2,1,0:T(8,128)S(1)} %get-tuple-element.22.ext, f32[2,2,256,128]{3,2,1,0:T(8,128)S(1)} %get-tuple-element.29.total, f32[2,256,128]{2,1,0:T(8,128)S(1)} %get-tuple-element.30.inverse, f32[256,128]{1,0:T(8,128)S(1)} %get-tuple-element.31.whole, ...), custom_call_target="tpu_custom_call" | custom-call | tf_op jit(solution)/shard_map/close/pallas_call | solution.py:521
Async XLA Ops:
  0.6 10.1 %copy-start.5 = (s32[2,1,1,16]{3,2,1,0:T(1,128)S(1)}, s32[2,1,1,16]{3,2,1,0:T(1,128)}, u32[]{:S(2)}) copy-start(s32[2,1,1,16]{3,2,1,0:T(1,128)} %param.10) | copy-start | bytes 388
  1.3 1.0 %copy-start = (f32[2,256,256]{2,1,0:T(8,128)S(1)}, f32[2,256,256]{2,1,0:T(8,128)}, u32[]{:S(2)}) copy-start(f32[2,256,256]{2,1,0:T(8,128)} %refs_4_.1) | copy-start | bytes 1572868
  2.3 8.4 %copy-start.1 = (bf16[1,1,16,128,128]{4,3,2,1,0:T(8,128)(2,1)S(1)}, bf16[1,1,16,128,128]{4,3,2,1,0:T(8,128)(2,1)}, u32[]{:S(2)}) copy-start(bf16[1,1,16,128,128]{4,3,2,1,0:T(8,128)(2,1)} %param.9) | copy-start | bytes 1572868
  2.3 8.4 %copy-start.2 = (f32[2,128,128]{2,1,0:T(8,128)S(1)}, f32[2,128,128]{2,1,0:T(8,128)}, u32[]{:S(2)}) copy-start(f32[2,128,128]{2,1,0:T(8,128)} %probe.3) | copy-start | bytes 393220
  2.3 8.5 %copy-start.3 = (bf16[256,256]{1,0:T(8,128)(2,1)S(1)}, bf16[256,256]{1,0:T(8,128)(2,1)}, u32[]{:S(2)}) copy-start(bf16[256,256]{1,0:T(8,128)(2,1)} %constant.5.clone.back) | copy-start | bytes 393220
  2.3 8.5 %copy-start.4 = (bf16[256,256]{1,0:T(8,128)(2,1)S(1)}, bf16[256,256]{1,0:T(8,128)(2,1)}, u32[]{:S(2)}) copy-start(bf16[256,256]{1,0:T(8,128)(2,1)} %constant.4.clone.ahead) | copy-start | bytes 393220
